TPU v7x, 32 devices: a whole 2x2x4 slice. The times are simulated.
32 devices in a mesh: rep: 4 (over y, x), fsdp: 8 (over z, core).
Axes of the slice: x: 2, y: 2, z: 4, core: 2. Of those that a mesh axis runs over, the one named last changes fastest.
Arguments:
- tokens: bfloat16 [64, 512, 768], P(('rep', 'fsdp')), may hold values from -6 to 6
- memory: bfloat16 [64, 1024, 768], P(('rep', 'fsdp')), may hold values from -6 to 6
- prefix_len: int32 [64], P(('rep', 'fsdp')), may hold values from 51 to 256
- bucket_table: int32 [1023], replicated, may hold values from 0 to 31
- rel_bias: bfloat16 [384], P('fsdp'), may hold values from -4 to 4
- gain_self: bfloat16 [768], P('fsdp'), may hold values from 0.5 to 1.5
- self_query: bfloat16 [768, 768], P('fsdp'), may hold values from -0.099609375 to 0.099609375
- self_key: bfloat16 [768, 768], P('fsdp'), may hold values from -0.099609375 to 0.099609375
- self_value: bfloat16 [768, 768], P('fsdp'), may hold values from -0.21875 to 0.21875
- self_out: bfloat16 [768, 768], P('fsdp'), may hold values from -0.875 to 0.875
- gain_cross: bfloat16 [768], P('fsdp'), may hold values from 0.5 to 1.5
- cross_query: bfloat16 [768, 768], P('fsdp'), may hold values from -0.099609375 to 0.099609375
- cross_key: bfloat16 [768, 768], P('fsdp'), may hold values from -0.099609375 to 0.099609375
- cross_value: bfloat16 [768, 768], P('fsdp'), may hold values from -0.21875 to 0.21875
- cross_out: bfloat16 [768, 768], P('fsdp'), may hold values from -1.25 to 1.25
- gain_feed: bfloat16 [768], P('fsdp'), may hold values from 0.5 to 1.5
- gate_weight: bfloat16 [768, 2048], P('fsdp'), may hold values from -0.21875 to 0.21875
- up_weight: bfloat16 [768, 2048], P('fsdp'), may hold values from -0.21875 to 0.21875
- down_weight: bfloat16 [2048, 768], P('fsdp'), may hold values from -0.25 to 0.25
- out_grad: bfloat16 [64, 512, 768], P(('rep', 'fsdp')), may hold values from -6 to 6
Outputs:
- layer_out: bfloat16 [64, 512, 768], P(('rep', 'fsdp'))
- tokens_grad: float32 [64, 512, 768], P(('rep', 'fsdp'))
- memory_grad: float32 [64, 1024, 768], P(('rep', 'fsdp'))
- rel_bias_grad: float32 [384], P('fsdp')
- gain_self_grad: float32 [768], P('fsdp')
- self_query_grad: float32 [768, 768], P('fsdp', 'rep')
- self_key_grad: float32 [768, 768], P('fsdp', 'rep')
- self_value_grad: float32 [768, 768], P('fsdp', 'rep')
- self_out_grad: float32 [768, 768], P('fsdp', 'rep')
- gain_cross_grad: float32 [768], P('fsdp')
- cross_query_grad: float32 [768, 768], P('fsdp', 'rep')
- cross_key_grad: float32 [768, 768], P('fsdp', 'rep')
- cross_value_grad: float32 [768, 768], P('fsdp', 'rep')
- cross_out_grad: float32 [768, 768], P('fsdp', 'rep')
- gain_feed_grad: float32 [768], P('fsdp')
- gate_weight_grad: float32 [768, 2048], P('fsdp', 'rep')
- up_weight_grad: float32 [768, 2048], P('fsdp', 'rep')
- down_weight_grad: float32 [2048, 768], P('fsdp', 'rep')
All inputs are finite; a program needn't handle non-finite values.
Results may differ from a plain program's by a relative error of at most 0.03.
Values may be sent and summed in bfloat16 or wider, within the bound.
A program may use at most 384 MiB of HBM per device.

v0:
```python
import functools

import jax
import jax.numpy as jnp
from jax import lax
from jax.experimental import pallas as pl
from jax.experimental.pallas import tpu as pltpu
from jax.sharding import PartitionSpec as P

NHEAD = 12
DHEAD = 64
BUCKETS = 32
PAIRS = NHEAD // 2
LANES = 2 * DHEAD
PREFIX_MAX = 256

EPSILON = 1e-06
CUBIC_TERM = 0.044715
SQRT_TWO_PI = 0.7978845608028654
NEGATIVE = -1000000000.0

F32 = jnp.float32
BF16 = jnp.bfloat16
LAST_DIMS = (((1,), (1,)), ((), ()))


def matmul(left_side, right_side):
    return jnp.dot(left_side, right_side, preferred_element_type=F32)


def back_term(gradient, weight):
    return lax.dot_general(gradient, weight, LAST_DIMS, preferred_element_type=F32)


def inverse_rms(values):
    return lax.rsqrt(jnp.mean(values * values, axis=-1, keepdims=True) + EPSILON)


def norm_back(values, scale_rows, gain_vec, upstream):
    weighted = upstream * gain_vec
    gain_grad = jnp.sum(upstream * values * scale_rows, axis=0)
    input_grad = scale_rows * weighted - values * scale_rows * scale_rows * scale_rows * jnp.mean(
        values * weighted, axis=-1, keepdims=True
    )
    return (input_grad, gain_grad)


def one_head(rows, head):
    lane = lax.broadcasted_iota(jnp.int32, rows.shape, 1)
    keep = lane < DHEAD if head == 0 else lane >= DHEAD
    return jnp.where(keep, rows, jnp.zeros_like(rows))


def flipped(rows):
    return rows.astype(F32).T.astype(BF16)


def tree(fold, rows, groups):
    step = rows.shape[0] // groups
    total = rows[:step]
    for index in range(1, groups):
        total = fold(total, rows[index * step : (index + 1) * step])
    return total


def column_max(rows, groups):
    return jnp.max(tree(jnp.maximum, rows, groups), axis=0, keepdims=True)


def column_sum(rows, groups):
    return jnp.sum(tree(jnp.add, rows, groups), axis=0, keepdims=True)


def allowed_at(shape, key_start, query_start, prefix):
    key = lax.broadcasted_iota(jnp.int32, shape, 0) + key_start
    query = lax.broadcasted_iota(jnp.int32, shape, 1) + query_start
    return (key <= query) | (key < prefix)


def skew_kernel(table_ref, buckets_ref, out_ref):
    bucket = lax.broadcasted_iota(jnp.int32, (BUCKETS, buckets_ref.shape[1]), 0)
    onehot = (bucket == buckets_ref[...]).astype(BF16)
    by_offset = matmul(table_ref[...], onehot)
    width = out_ref.shape[2]
    total = by_offset.shape[1]
    for head in range(NHEAD):
        rows = jnp.broadcast_to(by_offset[head : head + 1], (LANES, total))
        rolled = pltpu.roll(rows, total - (LANES - 1), 1, stride=1, stride_axis=0)
        out_ref[head] = rolled[:, :width]


def skewed_bias(table, buckets_back, length):
    total = 2 * length
    return pl.pallas_call(
        skew_kernel,
        out_shape=jax.ShapeDtypeStruct((NHEAD, LANES, total - LANES), F32),
        name="skewed_bias",
    )(jnp.pad(table, ((0, 4), (0, 0))), buckets_back)


HEADROOM = 70.0


def self_forward(prefix_ref, query_ref, key_ref, value_ref, bias_ref, out_ref, lse_ref):
    length = query_ref.shape[0]
    block = 256
    prefix = prefix_ref[pl.program_id(0)]
    queries = query_ref[...]
    keys = key_ref[...]
    values = flipped(value_ref[...])

    def run(exact):
        excess = jnp.zeros((1, block), F32)
        for start in range(0, length, block):
            stop = start + block
            count = max(PREFIX_MAX, stop)
            outs = []
            for head in range(2):
                scores = back_term(keys[:count], one_head(queries[start:stop], head))
                parts = []
                for base in range(0, count, LANES):
                    shift = length - LANES - base + start
                    part = scores[base : base + LANES] + bias_ref[head, :, shift : shift + block]
                    if base + LANES - 1 > start:
                        part = jnp.where(
                            allowed_at(part.shape, base, start, prefix), part, NEGATIVE
                        )
                    parts.append(part)
                top = parts[0]
                for part in parts[1:]:
                    top = jnp.maximum(top, part)
                top = column_max(top, 4)
                anchor = top if exact else column_max(parts[0], 4)
                if not exact:
                    excess = jnp.maximum(excess, top - anchor)
                shares = [jnp.exp(part - anchor) for part in parts]
                total = shares[0]
                for share in shares[1:]:
                    total = total + share
                total = column_sum(total, 4)
                share = jnp.concatenate([item.astype(BF16) for item in shares], axis=0)
                context = matmul(values[head * DHEAD : (head + 1) * DHEAD, :count], share)
                outs.append(context * (1.0 / total))
                lse_ref[head : head + 1, start:stop] = anchor + jnp.log(total)
            out_ref[start:stop, :] = jnp.concatenate(outs, axis=0).T.astype(BF16)
        return jnp.max(excess)

    excess = run(False)

    @pl.when(excess > HEADROOM)
    def _():
        run(True)


def cross_forward(query_ref, key_ref, value_ref, out_ref, lse_ref):
    keys = key_ref[...]
    values = flipped(value_ref[...])
    queries = query_ref[...]

    def run(exact):
        excess = jnp.zeros((1, queries.shape[0]), F32)
        ahead = [back_term(keys, one_head(queries, head)) for head in range(2)]
        outs = []
        for head in range(2):
            scores = ahead[head]
            top = column_max(scores, 16)
            anchor = top if exact else column_max(scores[: 2 * LANES], 8)
            if not exact:
                excess = jnp.maximum(excess, top - anchor)
            share = jnp.exp(scores - anchor)
            total = column_sum(share, 16)
            context = matmul(values[head * DHEAD : (head + 1) * DHEAD], share.astype(BF16))
            outs.append(context * (1.0 / total))
            lse_ref[head : head + 1, :] = anchor + jnp.log(total)
        out_ref[...] = jnp.concatenate(outs, axis=0).T.astype(BF16)
        return jnp.max(excess)

    excess = run(False)

    @pl.when(excess > HEADROOM)
    def _():
        run(True)


def cross_backward(
    query_ref, key_ref, value_ref, up_ref, context_ref, lse_ref, dq_ref, dk_ref, dv_ref
):
    length = query_ref.shape[0]
    block = 256
    keys = key_ref[...]
    values = value_ref[...]
    queries = query_ref[...]
    upstream = up_ref[...]
    keys_flipped = flipped(keys)
    inner = (upstream.astype(F32) * context_ref[...].astype(F32)).T
    key_grad = None
    value_grad = None
    for start in range(0, length, block):
        rows = slice(start, start + block)
        grads = []
        for head in range(2):
            sub = slice(head * DHEAD, (head + 1) * DHEAD)
            query = one_head(queries[rows], head)
            above = one_head(upstream[rows], head)
            row_inner = jnp.sum(inner[sub, rows], axis=0, keepdims=True)
            shares = jnp.exp(back_term(keys, query) - lse_ref[head : head + 1, rows])
            share_grad = back_term(values, above)
            score_grad = (shares * (share_grad - row_inner)).astype(BF16)
            value_part = matmul(shares.astype(BF16), above)
            key_part = matmul(score_grad, query)
            value_grad = value_part if value_grad is None else value_grad + value_part
            key_grad = key_part if key_grad is None else key_grad + key_part
            grads.append(matmul(keys_flipped[sub], score_grad))
        dq_ref[rows, :] = jnp.concatenate(grads, axis=0).T.astype(BF16)
    dk_ref[...] = key_grad.astype(BF16)
    dv_ref[...] = value_grad.astype(BF16)


def self_backward(
    prefix_ref,
    query_ref,
    key_ref,
    value_ref,
    up_ref,
    context_ref,
    lse_ref,
    bias_ref,
    dq_ref,
    dk_ref,
    dv_ref,
    diag_ref,
    acc_ref,
):
    length = query_ref.shape[0]
    block = 256
    step = pl.program_id(1)
    prefix = prefix_ref[step]

    @pl.when(step == 0)
    def _():
        acc_ref[...] = jnp.zeros_like(acc_ref)

    queries = query_ref[...]
    keys = key_ref[...]
    values = value_ref[...]
    upstream = up_ref[...]
    keys_flipped = flipped(keys)
    inner = (upstream.astype(F32) * context_ref[...].astype(F32)).T
    count_all = length // block
    key_grad = [None] * count_all
    value_grad = [None] * count_all
    for start in range(0, length, block):
        stop = start + block
        count = max(PREFIX_MAX, stop)
        rows = slice(start, stop)
        grads = []
        for head in range(2):
            sub = slice(head * DHEAD, (head + 1) * DHEAD)
            query = one_head(queries[rows], head)
            above = one_head(upstream[rows], head)
            row_inner = jnp.sum(inner[sub, rows], axis=0, keepdims=True)
            row_lse = lse_ref[head : head + 1, rows]
            scores = back_term(keys[:count], query)
            share_grad = back_term(values[:count], above)
            shares = []
            score_grads = []
            for base in range(0, count, LANES):
                part = slice(base, base + LANES)
                shift = length - LANES - base + start
                share = jnp.exp(
                    scores[part] + bias_ref[head, :, shift : shift + block] - row_lse
                )
                if base + LANES - 1 > start:
                    share = jnp.where(allowed_at(share.shape, base, start, prefix), share, 0.0)
                score_grad = share * (share_grad[part] - row_inner)
                acc_ref[head, :, shift : shift + block] += score_grad
                shares.append(share.astype(BF16))
                score_grads.append(score_grad.astype(BF16))
            share = jnp.concatenate(shares, axis=0)
            score_grad = jnp.concatenate(score_grads, axis=0)
            value_part = matmul(share, above)
            key_part = matmul(score_grad, query)
            for index in range(count // block):
                part = slice(index * block, (index + 1) * block)
                if value_grad[index] is None:
                    value_grad[index] = value_part[part]
                    key_grad[index] = key_part[part]
                else:
                    value_grad[index] = value_grad[index] + value_part[part]
                    key_grad[index] = key_grad[index] + key_part[part]
            grads.append(matmul(keys_flipped[sub, :count], score_grad))
        dq_ref[rows, :] = jnp.concatenate(grads, axis=0).T.astype(BF16)
    for index in range(count_all):
        part = slice(index * block, (index + 1) * block)
        dk_ref[part, :] = key_grad[index].astype(BF16)
        dv_ref[part, :] = value_grad[index].astype(BF16)

    @pl.when(step == pl.num_programs(1) - 1)
    def _():
        total = 2 * length
        for head in range(2):
            rows = jnp.concatenate([acc_ref[head], jnp.zeros((LANES, LANES), F32)], axis=1)
            half = LANES // 2
            while half >= 1:
                rows = rows[:half] + pltpu.roll(rows[half:], total - half, 1)
                half //= 2
            diag_ref[head : head + 1, :] = pltpu.roll(rows, LANES - 1, 1)


def spec(shape, index):
    return pl.BlockSpec(shape, index)


def run_self_forward(prefix, qkv, bias, nseq):
    length = qkv.shape[0] // nseq
    return pl.pallas_call(
        self_forward,
        grid_spec=pltpu.PrefetchScalarGridSpec(
            num_scalar_prefetch=1,
            grid=(nseq, PAIRS),
            in_specs=[
                spec((length, LANES), lambda s, p, _: (s, p)),
                spec((length, LANES), lambda s, p, _: (s, PAIRS + p)),
                spec((length, LANES), lambda s, p, _: (s, 2 * PAIRS + p)),
                spec((2, LANES, 2 * length - LANES), lambda s, p, _: (p, 0, 0)),
            ],
            out_specs=[
                spec((length, LANES), lambda s, p, _: (s, p)),
                spec((None, None, 2, length), lambda s, p, _: (s, p, 0, 0)),
            ],
        ),
        out_shape=[
            jax.ShapeDtypeStruct((qkv.shape[0], PAIRS * LANES), BF16),
            jax.ShapeDtypeStruct((nseq, PAIRS, 2, length), F32),
        ],
        cost_estimate=pl.CostEstimate(
            flops=20_000_000_000, bytes_accessed=12_000_000, transcendentals=0
        ),
        name="self_forward",
    )(prefix, qkv, qkv, qkv, bias)


def run_cross_forward(query, kv, nseq):
    length = query.shape[0] // nseq
    count = kv.shape[0] // nseq
    return pl.pallas_call(
        cross_forward,
        grid=(nseq, PAIRS),
        in_specs=[
            spec((length, LANES), lambda s, p: (s, p)),
            spec((count, LANES), lambda s, p: (s, p)),
            spec((count, LANES), lambda s, p: (s, PAIRS + p)),
        ],
        out_specs=[
            spec((length, LANES), lambda s, p: (s, p)),
            spec((None, None, 2, length), lambda s, p: (s, p, 0, 0)),
        ],
        out_shape=[
            jax.ShapeDtypeStruct(query.shape, BF16),
            jax.ShapeDtypeStruct((nseq, PAIRS, 2, length), F32),
        ],
        cost_estimate=pl.CostEstimate(
            flops=24_000_000_000, bytes_accessed=10_000_000, transcendentals=0
        ),
        name="cross_forward",
    )(query, kv, kv)


def run_cross_backward(query, kv, upstream, context, lse, nseq):
    length = query.shape[0] // nseq
    count = kv.shape[0] // nseq
    rows = spec((length, LANES), lambda s, p: (s, p))
    wide = spec((count, LANES), lambda s, p: (s, p))
    return pl.pallas_call(
        cross_backward,
        grid=(nseq, PAIRS),
        in_specs=[
            rows,
            wide,
            spec((count, LANES), lambda s, p: (s, PAIRS + p)),
            rows,
            rows,
            spec((None, None, 2, length), lambda s, p: (s, p, 0, 0)),
        ],
        out_specs=[rows, wide, wide],
        out_shape=[
            jax.ShapeDtypeStruct(query.shape, BF16),
            jax.ShapeDtypeStruct((kv.shape[0], PAIRS * LANES), BF16),
            jax.ShapeDtypeStruct((kv.shape[0], PAIRS * LANES), BF16),
        ],
        cost_estimate=pl.CostEstimate(
            flops=36_000_000_000, bytes_accessed=20_000_000, transcendentals=0
        ),
        name="cross_backward",
    )(query, kv, kv, upstream, context, lse)


def run_self_backward(prefix, qkv, upstream, context, lse, bias, nseq):
    length = qkv.shape[0] // nseq
    rows = spec((length, LANES), lambda p, s, _: (s, p))
    return pl.pallas_call(
        self_backward,
        grid_spec=pltpu.PrefetchScalarGridSpec(
            num_scalar_prefetch=1,
            grid=(PAIRS, nseq),
            in_specs=[
                rows,
                spec((length, LANES), lambda p, s, _: (s, PAIRS + p)),
                spec((length, LANES), lambda p, s, _: (s, 2 * PAIRS + p)),
                rows,
                rows,
                spec((None, None, 2, length), lambda p, s, _: (s, p, 0, 0)),
                spec((2, LANES, 2 * length - LANES), lambda p, s, _: (p, 0, 0)),
            ],
            out_specs=[
                rows,
                rows,
                rows,
                spec((None, 2, 2 * length), lambda p, s, _: (p, 0, 0)),
            ],
            scratch_shapes=[pltpu.VMEM((2, LANES, 2 * length - LANES), F32)],
        ),
        out_shape=[jax.ShapeDtypeStruct(upstream.shape, BF16)] * 3
        + [jax.ShapeDtypeStruct((PAIRS, 2, 2 * length), F32)],
        cost_estimate=pl.CostEstimate(
            flops=24_000_000_000, bytes_accessed=20_000_000, transcendentals=0
        ),
        name="self_backward",
    )(prefix, qkv, qkv, qkv, upstream, context, lse, bias)


FEED_BLOCK = 256


def feed_kernel(
    middle_ref,
    context_ref,
    out_proj_ref,
    gain_ref,
    up_grad_ref,
    gate_ref,
    up_ref,
    down_ref,
    result_ref,
    later_grad_ref,
    branch_ref,
    context_grad_ref,
    gain_grad_ref,
    down_term_ref,
    pair_term_ref,
    later_ref,
    normed_ref,
    flipped_ref,
    result_acc,
    third_acc,
):
    step = pl.program_id(0)
    count = middle_ref.shape[0]
    chunk = 256
    chunks = [slice(start, start + chunk) for start in range(0, count, chunk)]

    @pl.when(step == 0)
    def _():
        for rows in chunks:
            later = middle_ref[rows] + matmul(context_ref[rows], out_proj_ref[...])
            normed = (later * inverse_rms(later) * gain_ref[...]).astype(BF16)
            later_ref[rows] = later
            normed_ref[rows] = normed
            flipped_ref[:, rows] = flipped(normed)
            result_acc[rows] = jnp.zeros_like(later)
            third_acc[rows] = jnp.zeros_like(later)

    gate_proj = gate_ref[...]
    up_proj = up_ref[...]
    down_proj = down_ref[...]
    hidden_flipped = []
    gate_grads = []
    lift_grads = []
    for rows in chunks:
        normed = normed_ref[rows]
        gate = matmul(normed, gate_proj)
        lift = matmul(normed, up_proj)
        hidden_grad = back_term(up_grad_ref[rows], down_proj)
        square = gate * gate
        tangent = jnp.tanh(SQRT_TWO_PI * gate * (1.0 + CUBIC_TERM * square))
        half = 0.5 * (1.0 + tangent)
        active = gate * half
        slope = half + 0.5 * gate * (1.0 - tangent * tangent) * (
            SQRT_TWO_PI + 3.0 * CUBIC_TERM * SQRT_TWO_PI * square
        )
        hidden = active * lift
        gate_grad = (hidden_grad * lift * slope).astype(BF16)
        lift_grad = (hidden_grad * active).astype(BF16)
        hidden_flipped.append(hidden.T.astype(BF16))
        gate_grads.append(gate_grad)
        lift_grads.append(lift_grad)
        result_acc[rows] += matmul(hidden.astype(BF16), down_proj)
        third_acc[rows] += back_term(gate_grad, gate_proj) + back_term(lift_grad, up_proj)
    hidden_flipped = jnp.concatenate(hidden_flipped, axis=1)
    down_term_ref[...] = matmul(hidden_flipped, up_grad_ref[...]).astype(BF16)
    gate_grads = jnp.concatenate(gate_grads, axis=0)
    lift_grads = jnp.concatenate(lift_grads, axis=0)
    pair_term_ref[:, :FEED_BLOCK] = matmul(flipped_ref[...], gate_grads).astype(BF16)
    pair_term_ref[:, FEED_BLOCK:] = matmul(flipped_ref[...], lift_grads).astype(BF16)

    @pl.when(step == pl.num_programs(0) - 1)
    def _():
        gain_grad = jnp.zeros(gain_ref.shape, F32)
        for rows in chunks:
            later = later_ref[rows]
            result_ref[rows] = (later + result_acc[rows]).astype(BF16)
            carry, part = norm_back(later, inverse_rms(later), gain_ref[...], third_acc[rows])
            gain_grad = gain_grad + part[None, :]
            later_grad = up_grad_ref[rows].astype(F32) + carry
            branch = later_grad.astype(BF16)
            later_grad_ref[rows] = later_grad
            branch_ref[rows] = branch
            context_grad_ref[rows] = back_term(branch, out_proj_ref[...]).astype(BF16)
        gain_grad_ref[...] = gain_grad


def run_feed(middle, context, out_proj, out_block, gain, upstream, gate_up, down):
    count, width = middle.shape
    ffn = down.shape[0]
    blocks = ffn // FEED_BLOCK

    def whole(shape, **extra):
        return pl.BlockSpec(shape, lambda j: (0, 0), **extra)

    once = {"pipeline_mode": pl.Buffered(1)}
    rows = (count, width)
    return pl.pallas_call(
        feed_kernel,
        grid=(blocks,),
        in_specs=[
            whole(rows, **once),
            whole(rows, **once),
            pl.BlockSpec((width, width), lambda j: (0, out_block), **once),
            whole((1, width)),
            whole(rows, **once),
            spec((width, FEED_BLOCK), lambda j: (0, j)),
            spec((width, FEED_BLOCK), lambda j: (0, blocks + j)),
            spec((FEED_BLOCK, width), lambda j: (j, 0)),
        ],
        out_specs=[
            whole(rows),
            whole(rows),
            whole(rows),
            whole(rows),
            whole((1, width)),
            spec((FEED_BLOCK, width), lambda j: (j, 0)),
            spec((width, 2 * FEED_BLOCK), lambda j: (0, j)),
        ],
        out_shape=[
            jax.ShapeDtypeStruct(rows, BF16),
            jax.ShapeDtypeStruct(rows, F32),
            jax.ShapeDtypeStruct(rows, BF16),
            jax.ShapeDtypeStruct(rows, BF16),
            jax.ShapeDtypeStruct((1, width), F32),
            jax.ShapeDtypeStruct((ffn, width), BF16),
            jax.ShapeDtypeStruct((width, 2 * ffn), BF16),
        ],
        scratch_shapes=[
            pltpu.VMEM(rows, F32),
            pltpu.VMEM(rows, BF16),
            pltpu.VMEM((width, count), BF16),
            pltpu.VMEM(rows, F32),
            pltpu.VMEM(rows, F32),
        ],
        cost_estimate=pl.CostEstimate(
            flops=32_000_000_000, bytes_accessed=40_000_000, transcendentals=0
        ),
        compiler_params=pltpu.CompilerParams(vmem_limit_bytes=60 << 20),
        name="feed",
    )(middle, context, out_proj, gain, upstream, gate_up, gate_up, down)


def close_kernel(count, project, *refs):
    values_ref, carry_ref, gain_ref, left_ref, right_ref = refs[:5]
    grad_refs = refs[5 : 5 + count]
    weight_refs = refs[5 + count : 5 + 2 * count]
    at = 5 + 2 * count
    if project:
        proj_ref = refs[at]
        at += 1
    out_ref, gain_grad_ref = refs[at : at + 2]
    term_refs = refs[at + 2 : at + 3 + count]
    at += 3 + count
    if project:
        branch_ref, projected_ref = refs[at : at + 2]
        at += 2
    sums = refs[at : at + 1 + count]
    gain_sum = refs[at + 1 + count]
    step = pl.program_id(0)

    @pl.when(step == 0)
    def _():
        gain_sum[...] = jnp.zeros_like(gain_sum)
        for total in sums:
            total[...] = jnp.zeros_like(total)

    values = values_ref[...].astype(F32)
    gain = gain_ref[...]
    scale = inverse_rms(values)
    normed = (values * scale * gain).T.astype(BF16)
    upstream = None
    for index in range(count):
        grad = grad_refs[index][...]
        sums[index][...] += matmul(normed, grad)
        part = back_term(grad, weight_refs[index][...])
        upstream = part if upstream is None else upstream + part
    sums[count][...] += matmul(flipped(left_ref[...]), right_ref[...])
    carry, part = norm_back(values, scale, gain, upstream)
    gain_sum[...] += part[None, :]
    result = carry_ref[...] + carry
    out_ref[...] = result
    if project:
        branch = result.astype(BF16)
        branch_ref[...] = branch
        projected_ref[...] = back_term(branch, proj_ref[...]).astype(BF16)

    @pl.when(step == pl.num_programs(0) - 1)
    def _():
        gain_grad_ref[...] = gain_sum[...]
        for term, total in zip(term_refs, sums):
            term[...] = total[...].astype(BF16)


def run_close(values, carry, gain, left, right, grads, weights, project, name):
    rows, width = values.shape
    count = len(grads)
    block = 512
    wide = spec((block, width), lambda i: (i, 0))

    def columns(index):
        return pl.BlockSpec((width, width), lambda i: (0, index), pipeline_mode=pl.Buffered(1))

    whole = [spec((1, width), lambda i: (0, 0))]
    square = [spec((width, width), lambda i: (0, 0))] * (count + 1)
    extra = [] if project is None else [project]
    out_shape = [
        jax.ShapeDtypeStruct((rows, width), F32),
        jax.ShapeDtypeStruct((1, width), F32),
    ] + [jax.ShapeDtypeStruct((width, width), BF16)] * (count + 1)
    out_shape += [jax.ShapeDtypeStruct((rows, width), BF16)] * (2 * len(extra))
    return pl.pallas_call(
        functools.partial(close_kernel, count, project is not None),
        grid=(rows // block,),
        in_specs=[wide, wide]
        + whole
        + [wide] * (2 + count)
        + [columns(index) for _, index in weights + extra],
        out_specs=[wide] + whole + square + [wide] * (2 * len(extra)),
        out_shape=out_shape,
        scratch_shapes=[pltpu.VMEM((width, width), F32)] * (count + 1)
        + [pltpu.VMEM((1, width), F32)],
        cost_estimate=pl.CostEstimate(
            flops=8_000_000_000, bytes_accessed=25_000_000, transcendentals=0
        ),
        compiler_params=pltpu.CompilerParams(vmem_limit_bytes=60 << 20),
        name=name,
    )(values, carry, gain, left, right, *grads, *[item for item, _ in weights + extra])


def memory_kernel(
    memory_ref, key_grad_ref, value_grad_ref, key_ref, value_ref, out_ref, *rest
):
    key_term_ref, value_term_ref, key_sum, value_sum = rest
    step = pl.program_id(0)

    @pl.when(step == 0)
    def _():
        key_sum[...] = jnp.zeros_like(key_sum)
        value_sum[...] = jnp.zeros_like(value_sum)

    rows = flipped(memory_ref[...])
    key_grad = key_grad_ref[...]
    value_grad = value_grad_ref[...]
    out_ref[...] = back_term(key_grad, key_ref[...]) + back_term(value_grad, value_ref[...])
    key_sum[...] += matmul(rows, key_grad)
    value_sum[...] += matmul(rows, value_grad)

    @pl.when(step == pl.num_programs(0) - 1)
    def _():
        key_term_ref[...] = key_sum[...].astype(BF16)
        value_term_ref[...] = value_sum[...].astype(BF16)


def run_memory(memory, key_grad, value_grad, weights, key_block, value_block):
    rows, width = memory.shape
    block = 1024
    wide = spec((block, width), lambda i: (i, 0))
    square = spec((width, width), lambda i: (0, 0))

    def columns(index):
        return pl.BlockSpec((width, width), lambda i: (0, index), pipeline_mode=pl.Buffered(1))

    return pl.pallas_call(
        memory_kernel,
        grid=(rows // block,),
        in_specs=[wide, wide, wide, columns(key_block), columns(value_block)],
        out_specs=[wide, square, square],
        out_shape=[
            jax.ShapeDtypeStruct((rows, width), F32),
            jax.ShapeDtypeStruct((width, width), BF16),
            jax.ShapeDtypeStruct((width, width), BF16),
        ],
        scratch_shapes=[pltpu.VMEM((width, width), F32)] * 2,
        cost_estimate=pl.CostEstimate(
            flops=10_000_000_000, bytes_accessed=18_000_000, transcendentals=0
        ),
        compiler_params=pltpu.CompilerParams(vmem_limit_bytes=60 << 20),
        name="memory_close",
    )(memory, key_grad, value_grad, weights, weights)


MESH = pl.DeviceIdType.MESH


class Place:
    def __init__(self, line):
        self.line = line
        rep = lax.axis_index("rep")
        fsdp = lax.axis_index("fsdp")
        self.rep = rep
        self.fsdp = fsdp
        self.y = rep // 2
        self.x = rep % 2
        self.z = fsdp // 2
        self.core = fsdp % 2
        self.x_rep = self.y * 2 + 1 - self.x
        self.y_rep = (1 - self.y) * 2 + self.x

    def at_x(self):
        return {"rep": self.x_rep, "fsdp": self.fsdp}

    def at_y(self):
        return {"rep": self.y_rep, "fsdp": self.fsdp}

    def at_partner(self):
        return {"rep": self.rep, "fsdp": self.z * 2 + 1 - self.core}

    def at_line(self, side):
        return {"rep": self.rep, "fsdp": self.fsdp + (2 if side == 0 else -2)}

    def has_next(self, side):
        return self.z < self.line - 1 if side == 0 else self.z > 0

    def has_last(self, side):
        return self.has_next(1 - side)

    def arrives(self, side, hop):
        if side == 0:
            return self.z - 1 - hop >= 0
        return self.z + 1 + hop <= self.line - 1

    def source(self, side, hop):
        return self.z - 1 - hop if side == 0 else self.z + 1 + hop

    def at_far(self):
        half = self.line // 2
        return {"rep": self.rep, "fsdp": (self.z + half) % self.line * 2 + self.core}

    def greet(self, wide=False):
        barrier = pltpu.get_barrier_semaphore()
        targets = [self.at_x(), self.at_y(), self.at_partner()]
        if wide:
            targets.append({"rep": 3 - self.rep, "fsdp": self.fsdp})
            targets.append(self.at_far())
        for target in targets:
            pl.semaphore_signal(barrier, inc=1, device_id=target, device_id_type=MESH)
        for side in range(2):

            @pl.when(self.has_next(side))
            def _():
                pl.semaphore_signal(
                    barrier, inc=1, device_id=self.at_line(side), device_id_type=MESH
                )

        count = len(targets)
        for side in range(2):
            count = count + jnp.where(self.has_next(side), 1, 0)
        pl.semaphore_wait(barrier, count)


def remote(source, target, send, recv, device):
    return pltpu.make_async_remote_copy(
        src_ref=source,
        dst_ref=target,
        send_sem=send,
        recv_sem=recv,
        device_id=device,
        device_id_type=MESH,
    )


class GatherShape:
    def __init__(self, parts, by_rows):
        self.rows = parts[0].shape[0]
        self.widths = [part.shape[1] for part in parts]
        self.starts = [sum(self.widths[:index]) for index in range(len(parts))]
        self.columns = sum(self.widths)
        self.by_rows = by_rows

    def full(self, ref, owner):
        return ref.at[pl.ds(pl.multiple_of(owner * self.rows, 32), self.rows)]

    def piece(self, ref, owner, part, half=None):
        base = owner * self.rows
        if self.by_rows:
            rows = self.rows // 4
            base = base + part * rows
        else:
            rows = self.rows
        if half is not None:
            rows = rows // 2
            base = base + half * rows
        row_slice = pl.ds(pl.multiple_of(base, 16), rows)
        if self.by_rows:
            return ref.at[row_slice]
        width = self.columns // 4
        return ref.at[row_slice, pl.ds(pl.multiple_of(part * width, LANES), width)]


def gather_sems(line):
    hops = line - 1
    return [pltpu.SemaphoreType.DMA((5, 2, 2, hops)), pltpu.SemaphoreType.DMA((4,))] + [
        pltpu.SemaphoreType.DMA((2, 2, hops))
    ]


def gather_steps(place, shape, src, own, dst, sems):
    hop_sem, own_sem, pair_sem = sems
    hops = place.line - 1
    me = place.fsdp

    def load(index):
        at = pl.ds(shape.starts[index], shape.widths[index])
        return pltpu.make_async_copy(src[index], own.at[:, at], own_sem.at[0])

    def loaded():
        return pltpu.make_async_copy(own, own, own_sem.at[0])

    def keep():
        return pltpu.make_async_copy(own, shape.full(dst, me), own_sem.at[1])

    def own_pair():
        return remote(
            own, shape.full(dst, me), own_sem.at[2], own_sem.at[3], place.at_partner()
        )

    def owner(side, hop):
        return place.source(side, hop) * 2 + place.core

    def line_first(side):
        return remote(
            shape.piece(own, 0, place.rep),
            shape.piece(dst, me, place.rep),
            hop_sem.at[0, 0, side, 0],
            hop_sem.at[0, 1, side, 0],
            place.at_line(side),
        )

    def moved(kind, side, hop, block, device):
        return remote(
            block, block, hop_sem.at[kind, 0, side, hop], hop_sem.at[kind, 1, side, hop], device
        )

    def line_next(side, hop):
        block = shape.piece(dst, owner(side, hop - 1), place.rep)
        return moved(0, side, hop, block, place.at_line(side))

    def line_arrival(side, hop):
        block = shape.piece(dst, owner(side, hop), place.rep)
        return moved(0, side, hop, block, place.at_line(side))

    def plane(axis, side, hop):
        block = shape.piece(dst, owner(side, hop), place.rep)
        return moved(1 + axis, side, hop, block, place.at_x() if axis == 0 else place.at_y())

    def cross(axis, side, hop):
        part = place.x_rep if axis == 1 else place.y_rep
        block = shape.piece(dst, owner(side, hop), part, 1 - axis)
        return moved(3 + axis, side, hop, block, place.at_x() if axis == 0 else place.at_y())

    def pair(side, hop):
        block = shape.full(dst, owner(side, hop))
        return remote(
            block, block, pair_sem.at[0, side, hop], pair_sem.at[1, side, hop], place.at_partner()
        )

    def each(fn):
        def run():
            for hop in range(hops):
                for side in range(2):
                    pl.when(place.arrives(side, hop))(functools.partial(fn, side, hop))

        return run

    def start():
        for index in range(len(src)):
            load(index).start()
        loaded().wait()
        for side in range(2):
            pl.when(place.has_next(side))(lambda side=side: line_first(side).start())
        own_pair().start()
        keep().start()

    def arrive(side, hop):
        line_arrival(side, hop).wait_recv()
        if hop + 1 < hops:
            pl.when(place.has_next(side))(lambda: line_next(side, hop + 1).start())
        plane(0, side, hop).start()
        plane(1, side, hop).start()

    def turn(side, hop):
        plane(0, side, hop).wait_recv()
        cross(1, side, hop).start()
        plane(1, side, hop).wait_recv()
        cross(0, side, hop).start()

    def hand(side, hop):
        cross(0, side, hop).wait_recv()
        cross(1, side, hop).wait_recv()
        pair(side, hop).start()

    def finish():
        def last(side, hop):
            pair(side, hop).wait()
            for axis in range(2):
                plane(axis, side, hop).wait_send()
                cross(axis, side, hop).wait_send()
            if hop + 1 < hops:
                pl.when(place.has_next(side))(lambda: line_next(side, hop + 1).wait_send())

        each(last)()
        for side in range(2):
            pl.when(place.has_next(side))(lambda side=side: line_first(side).wait_send())
        own_pair().wait()
        keep().wait()

    return start, each(arrive), each(turn), each(hand), finish


def gather_kernel(shapes, line, *refs):
    count = len(shapes)
    sources = []
    at = 0
    for shape in shapes:
        sources.append(refs[at : at + len(shape.widths)])
        at += len(shape.widths)
    targets = refs[at : at + count]
    scratch = refs[at + count :]
    place = Place(line)
    place.greet()
    plans = []
    for index, shape in enumerate(shapes):
        own, *sems = scratch[4 * index : 4 * index + 4]
        plans.append(gather_steps(place, shape, sources[index], own, targets[index], sems))
    for stage in range(5):
        for plan in plans:
            plan[stage]()


def fast_gather(groups, line, by_rows, collective_id):
    shapes = [GatherShape(group, flag) for group, flag in zip(groups, by_rows)]
    scratch = []
    for shape in shapes:
        scratch.append(pltpu.VMEM((shape.rows, shape.columns), BF16))
        scratch.extend(gather_sems(line))
    anywhere = pl.BlockSpec(memory_space=pl.ANY)
    blocks = [block for group in groups for block in group]
    return pl.pallas_call(
        functools.partial(gather_kernel, shapes, line),
        in_specs=[anywhere] * len(blocks),
        out_specs=[anywhere] * len(groups),
        out_shape=[
            jax.ShapeDtypeStruct((2 * line * s.rows, s.columns), BF16) for s in shapes
        ],
        scratch_shapes=scratch,
        compiler_params=pltpu.CompilerParams(collective_id=collective_id, has_side_effects=True),
        name="fast_gather",
    )(*blocks)


class ReduceShape:
    def __init__(self, kind, rows, columns, sources):
        self.kind = kind
        self.rows = rows
        self.sources = sources
        if kind == "rows":
            self.block = (rows // 8, columns)
        elif kind == "pair":
            self.block = (rows // 2, columns // 2)
        else:
            self.block = (rows // 2, columns)
        self.exchange = kind != "pair"
        self.part_rows = rows // 4 if kind == "rows" else rows
        self.part_columns = columns // 4

    def pieces(self, refs, owner, half, quarter):
        rows, columns = self.block
        if self.kind == "rows":
            base = owner * self.rows + quarter * (self.rows // 4) + half * rows
            return [(refs[0].at[pl.ds(pl.multiple_of(base, 16), rows)], 0, columns)]
        at = pl.ds(pl.multiple_of(owner * self.rows + half * rows, 16), rows)
        if self.kind == "four":
            return [(refs[quarter].at[at], 0, columns)]
        width = columns // 2
        cut = slice(quarter * width, (quarter + 1) * width)
        return [(refs[index].at[at, cut], index * width, width) for index in range(2)]

    def out_shape(self):
        if self.exchange:
            return jax.ShapeDtypeStruct((4, self.part_rows, self.part_columns), F32)
        return jax.ShapeDtypeStruct((self.rows, self.block[1]), F32)

    def scratch(self, line):
        rows, columns = self.block
        dma = pltpu.SemaphoreType.DMA
        buffers = [
            pltpu.VMEM((line, 8, rows, columns), BF16),
            pltpu.VMEM((line, 8, rows, columns), BF16),
            pltpu.VMEM((line, 2, 2, rows, columns), BF16),
            pltpu.VMEM((line, 2, rows, columns), BF16),
            pltpu.VMEM((line, 2, rows, columns), BF16),
            pltpu.VMEM((2, line, 2, rows, columns), BF16),
            pltpu.VMEM((4, self.part_rows, self.part_columns), F32),
            pltpu.VMEM((4, self.part_rows, self.part_columns), F32),
            dma((line,)),
            dma((2, line)),
            dma((2, line, 2)),
            dma((2, line, 2)),
            dma((2, 2, line)),
            dma((2, 3)),
        ]
        return buffers


REDUCE_SCRATCH = 14


def added(left, right):
    return (left.astype(F32) + right.astype(F32)).astype(BF16)


def reduce_steps(place, shape, refs, out, scratch):
    own, other, first_in, second_in, total, line_in, parts, gathered = scratch[:8]
    load_sem, pair_sem, first_sem, second_sem, line_sem, swap_sem = scratch[8:]
    line = place.line
    near = (place.x, place.y)
    far = (place.y, place.x)
    near_device = (place.at_x(), place.at_y())
    far_device = (place.at_y(), place.at_x())

    def quarter_of(half, index):
        high, low = index // 2, index % 2
        return low * 2 + high if half == 0 else high * 2 + low

    def start(z):
        for half in range(2):
            for index in range(4):
                quarter = quarter_of(half, index)
                slot = half * 4 + index
                mine = shape.pieces(refs, 2 * z + place.core, half, quarter)
                theirs = shape.pieces(refs, 2 * z + 1 - place.core, half, quarter)
                for (view, column, width), (view_two, _, _) in zip(mine, theirs):
                    cut = pl.ds(column, width)
                    remote(
                        view_two,
                        other.at[z, slot, :, cut],
                        pair_sem.at[0, z],
                        pair_sem.at[1, z],
                        place.at_partner(),
                    ).start()
                    pltpu.make_async_copy(
                        view, own.at[z, slot, :, cut], load_sem.at[z]
                    ).start()

    def pair_all(z):
        return remote(
            own.at[z], other.at[z], pair_sem.at[0, z], pair_sem.at[1, z], place.at_partner()
        )

    def first(z, half):
        return remote(
            own.at[z, pl.ds(half * 4 + (1 - near[half]) * 2, 2)],
            first_in.at[z, half],
            first_sem.at[0, z, half],
            first_sem.at[1, z, half],
            near_device[half],
        )

    def second(z, half):
        return remote(
            own.at[z, half * 4 + near[half] * 2 + 1 - far[half]],
            second_in.at[z, half],
            second_sem.at[0, z, half],
            second_sem.at[1, z, half],
            far_device[half],
        )

    def along(z, side):
        return remote(
            total.at[z],
            line_in.at[side, z],
            line_sem.at[0, side, z],
            line_sem.at[1, side, z],
            place.at_line(side),
        )

    def pair_add(z):
        pltpu.make_async_copy(own.at[z], own.at[z], load_sem.at[z]).wait()
        pair_all(z).wait_recv()

        @pl.loop(0, 8)
        def _(slot):
            own[z, slot] = added(own[z, slot], other[z, slot])

        for half in range(2):
            first(z, half).start()

    def first_add(z):
        for half in range(2):
            first(z, half).wait_recv()
            base = half * 4 + near[half] * 2

            @pl.loop(0, 2)
            def _(index):
                own[z, base + index] = added(own[z, base + index], first_in[z, half, index])

            second(z, half).start()

    def second_add(z):
        for half in range(2):
            second(z, half).wait_recv()
            mine = half * 4 + near[half] * 2 + far[half]
            total[z, half] = added(own[z, mine], second_in[z, half])

    def line_send(z, side):
        ahead = place.z < z if side == 0 else place.z > z

        @pl.when(ahead)
        def _():
            @pl.when(place.has_last(side))
            def _():
                along(z, side).wait_recv()

                @pl.loop(0, 2)
                def _(half):
                    total[z, half] = added(total[z, half], line_in[side, z, half])

            along(z, side).start()

    def line_end(z):
        @pl.when(place.z == z)
        def _():
            for side in range(2):
                pl.when(place.has_last(side))(lambda: along(z, side).wait_recv())

    def swap(rep_slot, device, index):
        return remote(
            parts.at[rep_slot],
            gathered.at[place.rep],
            swap_sem.at[0, index],
            swap_sem.at[1, index],
            device,
        )

    def swaps():
        corner = 3 - place.rep
        return [
            swap(place.x_rep, place.at_x(), 0),
            swap(place.y_rep, place.at_y(), 1),
            swap(corner, {"rep": corner, "fsdp": place.fsdp}, 2),
        ]

    def finish():
        rows, columns = shape.block
        me = place.z
        for half in range(2):
            result = total[me, half].astype(F32)
            for side in range(2):
                extra = line_in[side, me, half].astype(F32)
                result = result + jnp.where(place.has_last(side), extra, 0.0)
            at = slice(half * rows, (half + 1) * rows)
            if shape.exchange:
                width = shape.part_columns
                for index in range(4):
                    parts[index, at, :] = result[:, index * width : (index + 1) * width]
            else:
                out[at, :] = result
        if shape.exchange:
            for copy in swaps():
                copy.start()
            gathered[place.rep] = parts[place.rep]

    def drain():
        if shape.exchange:
            for copy in swaps():
                copy.wait()
            out[...] = gathered[...]
        for z in range(line):
            pair_all(z).wait_send()
            for half in range(2):
                first(z, half).wait_send()
                second(z, half).wait_send()
            for side in range(2):
                ahead = place.z < z if side == 0 else place.z > z
                pl.when(ahead)(lambda: along(z, side).wait_send())

    order = [line - 1, 0] + [z for z in range(line - 2, 0, -1)]

    def begin():
        for z in order:
            start(z)

    def pairs():
        for z in order:
            pair_add(z)

    def firsts():
        for z in order:
            first_add(z)

    def seconds():
        for index, z in enumerate(order):
            second_add(z)
            if index > 0:
                line_send(order[index - 1], 0)
                line_send(order[index - 1], 1)
        line_send(order[-1], 0)
        line_send(order[-1], 1)

    def close():
        for z in range(line):
            line_end(z)
        finish()

    return begin, pairs, firsts, seconds, close, drain


class VectorSum:
    def __init__(self, place, source, out, scratch):
        self.place = place
        self.source = source
        self.out = out
        self.current, self.incoming, self.sems = scratch
        side = place.z % 2
        near = place.fsdp + 2 - 4 * side
        self.devices = [
            place.at_partner(),
            place.at_x(),
            place.at_y(),
            {"rep": place.rep, "fsdp": near},
            place.at_far(),
        ]

    @staticmethod
    def scratch(shape):
        return [
            pltpu.VMEM((6,) + shape, F32),
            pltpu.VMEM((5,) + shape, F32),
            pltpu.SemaphoreType.DMA((2, 5)),
        ]

    def copy(self, index):
        return remote(
            self.current.at[index],
            self.incoming.at[index],
            self.sems.at[0, index],
            self.sems.at[1, index],
            self.devices[index],
        )

    def round(self, index):
        if index == 0:
            self.current[0] = self.source[...]
        else:
            self.copy(index - 1).wait_recv()
            self.current[index] = self.current[index - 1] + self.incoming[index - 1]
        if index < 5:
            self.copy(index).start()

    def finish(self):
        self.out[...] = self.current[5]
        for index in range(5):
            self.copy(index).wait_send()


def reduce_kernel(shapes, line, vector_count, *refs):
    sources = []
    at = 0
    for shape in shapes:
        sources.append(refs[at : at + shape.sources])
        at += shape.sources
    vector_refs = refs[at : at + vector_count]
    at += vector_count
    outs = refs[at : at + len(shapes)]
    at += len(shapes)
    vector_outs = refs[at : at + vector_count]
    at += vector_count
    place = Place(line)
    place.greet(wide=True)
    plans = []
    for index, shape in enumerate(shapes):
        part = refs[at : at + REDUCE_SCRATCH]
        at += REDUCE_SCRATCH
        plans.append(reduce_steps(place, shape, sources[index], outs[index], part))
    vectors = []
    if vector_count:
        vectors = [VectorSum(place, vector_refs[0], vector_outs[0], refs[at : at + 3])]

    def rounds(*indices):
        for vector in vectors:
            for index in indices:
                vector.round(index)

    rounds(0)
    for plan in plans:
        plan[0]()
    plans[0][1]()
    rounds(1)
    plans[0][2]()
    rounds(2)
    for index, plan in enumerate(plans):
        ahead = plans[index + 1] if index + 1 < len(plans) else None
        if ahead is not None:
            ahead[1]()
        plan[3]()
        if ahead is not None:
            ahead[2]()
    rounds(3)
    for plan in plans:
        plan[4]()
    rounds(4, 5)
    for plan in plans:
        plan[5]()
    for vector in vectors:
        vector.finish()


def fast_reduce(groups, kinds, line, collective_id, vector=None):
    shapes = []
    blocks = []
    scratch = []
    for group, kind in zip(groups, kinds):
        rows, columns = group[0].shape
        shape = ReduceShape(kind, rows // (2 * line), columns, len(group))
        shapes.append(shape)
        blocks.extend(group)
        scratch.extend(shape.scratch(line))
    anywhere = pl.BlockSpec(memory_space=pl.ANY)
    local = pl.BlockSpec(memory_space=pltpu.VMEM)
    in_specs = [anywhere] * len(blocks)
    out_shape = [shape.out_shape() for shape in shapes]
    if vector is not None:
        blocks.append(vector)
        in_specs.append(local)
        out_shape.append(jax.ShapeDtypeStruct(vector.shape, F32))
        scratch.extend(VectorSum.scratch(vector.shape))
    return pl.pallas_call(
        functools.partial(reduce_kernel, shapes, line, 0 if vector is None else 1),
        in_specs=in_specs,
        out_specs=[local] * len(out_shape),
        out_shape=out_shape,
        scratch_shapes=scratch,
        compiler_params=pltpu.CompilerParams(
            collective_id=collective_id, has_side_effects=True, vmem_limit_bytes=60 << 20
        ),
        name="fast_reduce",
    )(*blocks)


PLANE = 4
CHIP = 2
LINE = 4


def small_plane():
    return lax.axis_size("rep") == PLANE and lax.axis_size("fsdp") == CHIP * LINE


def gather(block):
    return lax.all_gather(block, "fsdp", axis=0, tiled=True)


def gather_all(groups, by_rows, collective_id):
    if small_plane():
        return fast_gather(groups, LINE, by_rows, collective_id)
    return [gather(jnp.concatenate(group, axis=1)) for group in groups]


def scatter(block):
    return lax.psum_scatter(block.astype(BF16), "fsdp", scatter_dimension=0, tiled=True)


def column_blocks(block):
    rows = block.shape[0]
    return block.reshape(rows, lax.axis_size("rep"), -1).swapaxes(0, 1)


def scatter_columns(parts):
    count = lax.axis_size("rep")
    rows = parts[0].shape[0]
    split = [part.reshape(rows, count, -1) for part in parts]
    joined = jnp.concatenate(split, axis=2).reshape(rows, -1)
    own = lax.psum_scatter(joined, "rep", scatter_dimension=1, tiled=True)
    sizes = [part.shape[1] // count for part in parts]
    outs = []
    start = 0
    for size in sizes:
        outs.append(own[:, start : start + size].astype(F32))
        start += size
    return outs


def scatter_last(groups, vector, collective_id):
    if small_plane():
        *outs, total = fast_reduce(
            groups, ["four"] * len(groups), LINE, collective_id, vector
        )
        return [[out[index] for index in range(4)] for out in outs], total
    outs = [scatter_columns([scatter(item) for item in group]) for group in groups]
    return outs, lax.psum(vector, ("rep", "fsdp"))


def body(
    tokens,
    memory,
    prefix_len,
    bucket_table,
    rel_bias,
    gain_self,
    self_query,
    self_key,
    self_value,
    self_out,
    gain_cross,
    cross_query,
    cross_key,
    cross_value,
    cross_out,
    gain_feed,
    gate_weight,
    up_weight,
    down_weight,
    out_grad,
):
    nseq, length, width = tokens.shape
    shard = gain_self.shape[0]
    groups = width // shard
    entries = rel_bias.shape[0]
    small = jnp.stack(
        [gain_self, gain_cross, gain_feed, jnp.pad(rel_bias, (0, shard - entries))], axis=1
    )
    small = jnp.pad(small, ((0, 0), (0, 2 * LANES - 4)))
    first, second, down = gather_all(
        [
            [self_query, self_key, self_value, small],
            [self_out, cross_query, cross_key, cross_value, cross_out, small],
            [down_weight],
        ],
        [False, False, True],
        1,
    )
    gate_up_own = jnp.concatenate([gate_weight, up_weight], axis=1)
    gate_up_own, first, second, down = lax.optimization_barrier(
        (gate_up_own, first, second, down)
    )
    gate_up = gather(gate_up_own)
    qkv_proj = first[:, : 3 * width]
    picks = jnp.eye(8, LANES, dtype=BF16)
    vectors = back_term(picks, first[:, 3 * width : 3 * width + LANES])
    gain_first = vectors[0:1]
    gain_second = vectors[1:2]
    gain_third = vectors[2:3]
    table = vectors[3].astype(BF16).reshape(groups, shard)[:, :entries]
    table = table.reshape(NHEAD, BUCKETS)
    out_self = second[:, :width]
    query_cross = second[:, width : 2 * width]
    kv_cross = second[:, 2 * width : 4 * width]

    buckets_back = jnp.pad(bucket_table[::-1], (0, 1)).reshape(1, 2 * length)
    bias = skewed_bias(table, buckets_back, length)

    rows = nseq * length
    start_rows = tokens.reshape(rows, width).astype(F32)
    memory_rows = memory.reshape(-1, width)
    upstream = out_grad.reshape(rows, width)

    scale_first = inverse_rms(start_rows)
    normed_first = (start_rows * scale_first * gain_first).astype(BF16)
    qkv = matmul(normed_first, qkv_proj).astype(BF16)
    context, lse_self = run_self_forward(prefix_len, qkv, bias, nseq)
    middle = start_rows + matmul(context, out_self)
    scale_second = inverse_rms(middle)
    normed_second = (middle * scale_second * gain_second).astype(BF16)
    query_two = matmul(normed_second, query_cross).astype(BF16)
    kv_two = matmul(memory_rows, kv_cross).astype(BF16)
    context_two, lse_cross = run_cross_forward(query_two, kv_two, nseq)
    (
        result,
        later_grad,
        branch_two,
        context_two_grad,
        gain_third_grad,
        down_term,
        pair_term,
    ) = run_feed(middle, context_two, second, 4, gain_third, upstream, gate_up, down)
    down_own = scatter(down_term)
    pair_own = scatter(pair_term)
    query_two_grad, key_two_grad, value_two_grad = run_cross_backward(
        query_two, kv_two, context_two_grad, context_two, lse_cross, nseq
    )
    (
        middle_grad,
        gain_second_grad,
        query_term,
        out_term,
        branch_one,
        context_grad,
    ) = run_close(
        middle,
        later_grad,
        gain_second,
        context_two,
        branch_two,
        [query_two_grad],
        [(second, 1)],
        (second, 0),
        "cross_close",
    )
    memory_grad, key_term, value_term = run_memory(
        memory_rows, key_two_grad, value_two_grad, second, 2, 3
    )
    cross_terms = [query_term, key_term, value_term, out_term]
    query_grad, key_grad, value_grad, diagonal = run_self_backward(
        prefix_len, qkv, context_grad, context, lse_self, bias, nseq
    )
    tokens_grad, gain_first_grad, *self_terms = run_close(
        tokens.reshape(rows, width),
        middle_grad,
        gain_first,
        context,
        branch_one,
        [query_grad, key_grad, value_grad],
        [(first, 0), (first, 1), (first, 2)],
        None,
        "self_close",
    )

    onehot = (
        buckets_back.reshape(-1, 1) == jnp.arange(BUCKETS, dtype=jnp.int32)[None, :]
    ).astype(F32)
    onehot = onehot * (jnp.arange(2 * length) < 2 * length - 1)[:, None]
    bias_grad = jnp.dot(
        diagonal.reshape(NHEAD, 2 * length), onehot, precision=lax.Precision.HIGHEST
    )
    bias_rows = jnp.pad(
        bias_grad.reshape(groups, entries), ((0, 0), (0, shard - entries))
    ).reshape(width)
    vector_block = jnp.pad(
        jnp.concatenate(
            [gain_first_grad, gain_second_grad, gain_third_grad, bias_rows[None]], axis=0
        ),
        ((0, 4), (0, 0)),
    )
    down_own, pair_own, memory_grad, self_terms = lax.optimization_barrier(
        (down_own, pair_own, memory_grad, self_terms)
    )
    down_split = column_blocks(down_own)
    pair_split = column_blocks(pair_own)
    down_split, pair_split, self_terms = lax.optimization_barrier(
        (down_split, pair_split, self_terms)
    )
    down_weight_grad = lax.psum_scatter(down_split, "rep").astype(F32)
    pair_grad = lax.psum_scatter(pair_split, "rep").astype(F32)
    pair_grad = pair_grad.reshape(shard, -1, 2, FEED_BLOCK)
    gate_weight_grad = pair_grad[:, :, 0].reshape(shard, -1)
    up_weight_grad = pair_grad[:, :, 1].reshape(shard, -1)
    (cross_out_grads, self_out_grads), totals = scatter_last(
        [cross_terms, self_terms], vector_block, 3
    )
    own = lax.dynamic_slice(
        totals, (0, lax.axis_index("fsdp") * shard), (totals.shape[0], shard)
    )
    return (
        result.reshape(tokens.shape),
        tokens_grad.reshape(tokens.shape),
        memory_grad.reshape(memory.shape),
        own[3, :entries],
        own[0],
        *self_out_grads,
        own[1],
        *cross_out_grads,
        own[2],
        gate_weight_grad,
        up_weight_grad,
        down_weight_grad,
    )


def solution(mesh):
    batch = P(("rep", "fsdp"), None, None)
    matrix = P("fsdp", None)
    vector = P("fsdp")
    split = P("fsdp", "rep")
    in_specs = (
        (batch, batch, P(("rep", "fsdp")), P(), vector, vector)
        + (matrix,) * 4
        + (vector,)
        + (matrix,) * 4
        + (vector,)
        + (matrix,) * 3
        + (batch,)
    )
    out_specs = (
        (batch, batch, batch, vector, vector)
        + (split,) * 4
        + (vector,)
        + (split,) * 4
        + (vector,)
        + (split,) * 3
    )
    return jax.shard_map(body, mesh=mesh, in_specs=in_specs, out_specs=out_specs, check_vma=False)
```

profile of v0, /device:TPU:0, one launch (start us, length us, event | category | flops | bytes accessed | tf_op | source)
XLA Modules:
  0.0 405.2 jit_solution(2457375505370387381)
XLA Ops:
  7.3 0.8 pad_bitcast_fusion
  8.0 0.7 pad_maximum_fusion.1
  8.8 0.6 pad.25.refs_3_.refs_9_
  9.5 2.0 pad_maximum_fusion
  11.5 63.3 %fast_gather.1 = (bf16[768,2560]{1,0:T(8,128)(2,1)}, bf16[768,4096]{1,0:T(8,128)(2,1)}, bf16[2048,768]{1,0:T(8,128)(2,1)}) custom-call(bf16[96,768]{1,0:T(8,128)(2,1)} %refs_0_.1, bf16[96,768]{1,0:T(8,128)(2,1)} %refs_1_.1, bf16[96,768]{1,0:T(8,128)(2,1)} %refs_2_.1, bf16[96,256]{1,0:T(8,128)(2,1)} %pad.25.refs_3_.refs_9_, bf16[96,768]{1,0:T(8,128)(2,1)} %refs_4_.1, ...), custom_call_target="tpu_custom_call" | custom-call | tf_op jit(solution)/shard_map/fast_gather/pallas_call | solution.py:973
  75.5 1.1 fusion.17
  78.2 4.9 %skewed_bias.1.bias_ref = f32[12,128,896]{2,1,0:T(8,128)} custom-call(bf16[16,32]{1,0:T(8,128)(2,1)} %pad.26.table_ref, s32[1,1024]{1,0:T(1,128)} %bitcast.74), custom_call_target="tpu_custom_call" | custom-call | tf_op jit(solution)/shard_map/skewed_bias/pallas_call | solution.py:94
  83.7 7.6 %convolution_convert_fusion.1.query_ref.key_ref.value_ref = bf16[1024,2304]{1,0:T(8,128)(2,1)} fusion(bf16[768,2560]{1,0:T(8,128)(2,1)} %get-tuple-element.77.refs_8_.refs_9_.refs_10_, bf16[1024,768]{1,0:T(8,128)(2,1)S(1)} %bitcast.66, f32[768]{0:T(1024)S(1)} %get-tuple-element.133, f32[1024]{0:T(1024)S(1)} %bitcast.77), kind=kOutput, calls=%fused_computation.2 | convolution fusion | flops 3629383680 | bytes 9837568 | tf_op jit(solution)/shard_map/dot_general | solution.py:28
  91.3 20.2 %self_forward.1 = (bf16[1024,768]{1,0:T(8,128)(2,1)}, f32[2,6,2,512]{3,2,1,0:T(2,128)}) custom-call(s32[2]{0:T(128)} %prefix_ref.3, bf16[1024,2304]{1,0:T(8,128)(2,1)} %convolution_convert_fusion.1.query_ref.key_ref.value_ref, bf16[1024,2304]{1,0:T(8,128)(2,1)} %convolution_convert_fusion.1.query_ref.key_ref.value_ref, ...), custom_call_target="tpu_custom_call" | custom-call | flops 20000000000 | bytes 12000000 | tf_op jit(solution)/shard_map/self_forward/pallas_call | solution.py:316
  111.5 3.3 multiply_reduce_fusion
  114.9 5.0 %convolution_convert_fusion.2.query_ref = bf16[1024,768]{1,0:T(8,128)(2,1)} fusion(f32[1024,768]{1,0:T(8,128)S(1)} %get-tuple-element.149.middle_ref.refs_0_, f32[768]{0:T(1024)S(1)} %get-tuple-element.132, f32[1024]{0:T(1024)S(1)} %add_rsqrt_fusion, bf16[768,4096]{1,0:T(8,128)(2,1)} %get-tuple-element.79.out_proj_ref.refs_6_.refs_7_.key_ref.value_ref), kind=kOutput, calls=%fused_computation.12 | convolution fusion | flops 1211105280 | bytes 5905408 | tf_op jit(solution)/shard_map/dot_general | solution.py:28
  119.9 8.6 %fusion.key_ref.value_ref = bf16[2048,1536]{1,0:T(8,128)(2,1)} fusion(bf16[2048,768]{1,0:T(8,128)(2,1)S(1)} %bitcast.82, bf16[768,4096]{1,0:T(8,128)(2,1)} %get-tuple-element.79.out_proj_ref.refs_6_.refs_7_.key_ref.value_ref), kind=kOutput, calls=%fused_computation.1 | convolution fusion | flops 4834983936 | bytes 11796480 | tf_op jit(solution)/shard_map/dot_general | solution.py:28
  128.5 20.4 %cross_forward.1 = (bf16[1024,768]{1,0:T(8,128)(2,1)}, f32[2,6,2,512]{3,2,1,0:T(2,128)}) custom-call(bf16[1024,768]{1,0:T(8,128)(2,1)} %convolution_convert_fusion.2.query_ref, bf16[2048,1536]{1,0:T(8,128)(2,1)} %fusion.key_ref.value_ref, bf16[2048,1536]{1,0:T(8,128)(2,1)} %fusion.key_ref.value_ref), custom_call_target="tpu_custom_call" | custom-call | flops 24000000000 | bytes 10000000 | tf_op jit(solution)/shard_map/cross_forward/pallas_call | solution.py:346
  148.9 46.7 %feed.1 = (bf16[1024,768]{1,0:T(8,128)(2,1)}, f32[1024,768]{1,0:T(8,128)}, bf16[1024,768]{1,0:T(8,128)(2,1)}, bf16[1024,768]{1,0:T(8,128)(2,1)}, f32[1,768]{1,0:...) custom-call(f32[1024,768]{1,0:T(8,128)} %copy-done.8, ...), custom_call_target="tpu_custom_call" | custom-call | flops 32000000000 | bytes 40000000 | tf_op jit(solution)/shard_map/feed/pallas_call | solution.py:532
  195.7 0.7 reduce-scatter.11.cloned.1.call-update
  196.4 36.3 %cross_backward.1 = (bf16[1024,768]{1,0:T(8,128)(2,1)}, bf16[2048,768]{1,0:T(8,128)(2,1)}, bf16[2048,768]{1,0:T(8,128)(2,1)}) custom-call(bf16[1024,768]{1,0:T(8,128)(2,1)} %convolution_convert_fusion.2.query_ref, bf16[2048,1536]{1,0:T(8,128)(2,1)} %fusion.key_ref.value_ref, bf16[2048,1536]{1,0:T(8,128)(2,1)} %fusion.key_ref.value_ref, ...), custom_call_target="tpu_custom_call" | custom-call | flops 35999997952 | bytes 20000000 | tf_op jit(solution)/shard_map/cross_backward/pallas_call | solution.py:374
  232.8 13.5 %cross_close.1 = (f32[1024,768]{1,0:T(8,128)}, f32[1,768]{1,0:T(1,128)}, bf16[768,768]{1,0:T(8,128)(2,1)}, bf16[768,768]{1,0:T(8,128)(2,1)}, bf16[1024,768]{1,0:T(8,128)(2,1)}, /*index=5*/bf16[1024,768]{1,0:T(8,128)(2,1)}) custom-call(f32[1024,768]{1,0:T(8,128)} %copy-done.8, f32[1024,768]{1,0:T(8,128)} %get-tuple-element.84.refs_1_, ...), custom_call_target="tpu_custom_call" | custom-call | flops 8000000000 | bytes 25000000 | tf_op jit(solution)/shard_map/cross_close/pallas_call | solution.py:646
  246.3 26.0 %self_backward.1 = (bf16[1024,768]{1,0:T(8,128)(2,1)}, bf16[1024,768]{1,0:T(8,128)(2,1)}, bf16[1024,768]{1,0:T(8,128)(2,1)}, f32[6,2,1024]{2,1,0:T(2,128)}) custom-call(s32[2]{0:T(128)} %prefix_ref.3, bf16[1024,2304]{1,0:T(8,128)(2,1)} %convolution_convert_fusion.1.query_ref.key_ref.value_ref, ...), custom_call_target="tpu_custom_call" | custom-call | flops 24000000000 | bytes 20000000 | tf_op jit(solution)/shard_map/self_backward/pallas_call | solution.py:401
  272.3 19.1 %self_close.1 = (f32[1024,768]{1,0:T(8,128)}, f32[1,768]{1,0:T(1,128)}, bf16[768,768]{1,0:T(8,128)(2,1)}, bf16[768,768]{1,0:T(8,128)(2,1)}, bf16[768,768]{1,0:T(8,128)(2,1)}, /*index=5*/bf16[768,768]{1,0:T(8,128)(2,1)}) custom-call(bf16[1024,768]{1,0:T(8,128)(2,1)} %bitcast.65, f32[1024,768]{1,0:T(8,128)} %get-tuple-element.89.refs_1_, ...), custom_call_target="tpu_custom_call" | custom-call | flops 8000000000 | bytes 25000000 | tf_op jit(solution)/shard_map/self_close/pallas_call | solution.py:646
  291.4 16.8 %memory_close.1 = (f32[2048,768]{1,0:T(8,128)}, bf16[768,768]{1,0:T(8,128)(2,1)}, bf16[768,768]{1,0:T(8,128)(2,1)}) custom-call(bf16[2048,768]{1,0:T(8,128)(2,1)} %bitcast.81, bf16[2048,768]{1,0:T(8,128)(2,1)} %get-tuple-element.99.key_grad_ref, bf16[2048,768]{1,0:T(8,128)(2,1)} %get-tuple-element.100.value_grad_ref, ...), custom_call_target="tpu_custom_call" | custom-call | flops 10000000000 | bytes 18000000 | tf_op jit(solution)/shard_map/memory_close/pallas_call | solution.py:698
  308.3 2.1 copy.68
  310.4 1.9 copy.59
  313.0 0.6 fusion.12
  313.8 0.6 select_maximum_fusion.refs_8_
  314.5 74.6 %fast_reduce.1 = (f32[4,96,192]{2,1,0:T(8,128)}, f32[4,96,192]{2,1,0:T(8,128)}, f32[8,768]{1,0:T(8,128)}) custom-call(bf16[768,768]{1,0:T(8,128)(2,1)} %get-tuple-element.107.refs_0_, bf16[768,768]{1,0:T(8,128)(2,1)} %get-tuple-element.108.refs_1_, bf16[768,768]{1,0:T(8,128)(2,1)} %get-tuple-element.109.refs_2_, ...), custom_call_target="tpu_custom_call" | custom-call | tf_op jit(solution)/shard_map/fast_reduce/pallas_call | solution.py:1362
  389.0 0.8 constant_dynamic-slice_fusion
  390.8 2.1 slice_bitcast_fusion
  392.9 1.6 bitcast_convert_fusion
  394.5 1.3 reshape.126
  395.8 1.2 slice_reduce_fusion
  397.0 0.7 copy.65
  397.7 0.7 copy.66
  (52 shorter events, 5.0 us)
Async XLA Ops:
  7.2 67.9 %copy-start = (bf16[2,512,768]{2,1,0:T(8,128)(2,1)S(1)}, bf16[2,512,768]{2,1,0:T(8,128)(2,1)}, u32[]{:S(2)}) copy-start(bf16[2,512,768]{2,1,0:T(8,128)(2,1)} %param.20) | copy-start | bytes 4718596
  7.2 70.2 %copy-start.3 = (s32[1023]{0:T(1024)S(1)}, s32[1023]{0:T(1024)}, u32[]{:S(2)}) copy-start(s32[1023]{0:T(1024)} %param.23) | copy-start | bytes 12280
  7.2 141.7 %all-gather.2.cloned.1.call-start = ((), (), s32[]{:S(2)}) async-start(), calls=%async_computation.4 | async-start | bytes 7077888 | tf_op jit(solution)/shard_map/all_gather | solution.py:1385
  74.9 233.4 %reduce-scatter.9.cloned.1.call-start = ((), (), s32[]{:S(2)}) async-start(), calls=%async_computation.5 | async-start | bytes 3538944 | tf_op jit(solution)/shard_map/reduce_scatter | solution.py:1395
  114.8 5.1 %copy-start.8 = (f32[1024,768]{1,0:T(8,128)}, f32[1024,768]{1,0:T(8,128)S(1)}, u32[]{:S(2)}) copy-start(f32[1024,768]{1,0:T(8,128)S(1)} %get-tuple-element.149.middle_ref.refs_0_) | copy-start | bytes 9437188
  114.8 5.0 %copy-start.7 = (bf16[2,1024,768]{2,1,0:T(8,128)(2,1)S(1)}, bf16[2,1024,768]{2,1,0:T(8,128)(2,1)}, u32[]{:S(2)}) copy-start(bf16[2,1024,768]{2,1,0:T(8,128)(2,1)} %param.21) | copy-start | bytes 9437188
  195.6 112.7 %reduce-scatter.11.cloned.1.call-start = ((), (), s32[]{:S(2)}) async-start(), calls=%async_computation.6 | async-start | bytes 7077888 | tf_op jit(solution)/shard_map/reduce_scatter | solution.py:1395
  196.4 196.5 %reduce-scatter.15.cloned.1.call-start = ((), (), s32[]{:S(2)}) async-start(), calls=%async_computation.8 | async-start | bytes 491520
  308.2 4.8 %copy-start.1 = (f32[6,2,1024]{2,1,0:T(2,128)S(1)}, f32[6,2,1024]{2,1,0:T(2,128)}, u32[]{:S(2)}) copy-start(f32[6,2,1024]{2,1,0:T(2,128)} %get-tuple-element.124) | copy-start | bytes 147460
  308.2 4.8 %copy-start.2 = (s32[1024]{0:T(1024)S(1)}, s32[1024]{0:T(1024)}, u32[]{:S(2)}) copy-start(s32[1024]{0:T(1024)} %pad.27) | copy-start | bytes 12292
  308.2 5.6 %copy-start.4 = (f32[1,768]{1,0:T(1,128)S(1)}, f32[1,768]{1,0:T(1,128)}, u32[]{:S(2)}) copy-start(f32[1,768]{1,0:T(1,128)} %get-tuple-element.123) | copy-start | bytes 9220
  308.2 5.6 %copy-start.5 = (f32[1,768]{1,0:T(1,128)S(1)}, f32[1,768]{1,0:T(1,128)}, u32[]{:S(2)}) copy-start(f32[1,768]{1,0:T(1,128)} %get-tuple-element.122) | copy-start | bytes 9220
  308.2 5.6 %copy-start.6 = (f32[1,768]{1,0:T(1,128)S(1)}, f32[1,768]{1,0:T(1,128)}, u32[]{:S(2)}) copy-start(f32[1,768]{1,0:T(1,128)} %get-tuple-element.121) | copy-start | bytes 9220
  312.3 82.2 %reduce-scatter.13.cloned.1.call-start = ((), (), s32[]{:S(2)}) async-start(), calls=%async_computation.7 | async-start | bytes 983040
Sparse Core Ops, SparseCore 0:
  75.0 62.7 all-gather.1
  195.8 38.7 reduce-scatter.8
  236.9 69.0 reduce-scatter.10
  312.5 24.6 reduce-scatter.14
  339.9 29.4 reduce-scatter.12
where the time goes:
time: 409 us; the launch traced here: 405 us
  Pallas kernels  342 us (84%)
  matrix products  26.3 us (6%)
  local copies, waits for them, and re-layouts  15.8 us (4%)
  between operations  14.3 us (3%)
  other arithmetic  5.36 us (1%)
    pallas_call x1, Pallas kernels, fast_reduce(): pl.pallas_call(functools.partial(reduce_kernel, shapes, line, 0 if vector...  74.6 us
    pallas_call x1, Pallas kernels, fast_gather(): pl.pallas_call(functools.partial(gather_kernel, shapes, line), in_specs=[...  63.3 us
    pallas_call x1, Pallas kernels, run_feed(): pl.pallas_call(feed_kernel, grid=(blocks,), in_specs=[whole(rows, **once)...  46.7 us
    pallas_call x1, Pallas kernels, run_cross_backward(): pl.pallas_call(cross_backward, grid=(nseq, PAIRS), in_specs=[rows, wide,...  36.3 us
    pallas_call x2, Pallas kernels, run_close(): pl.pallas_call(functools.partial(close_kernel, count, project is not None...  32.6 us
    pallas_call x1, Pallas kernels, run_self_backward(): pl.pallas_call(self_backward, grid_spec=pltpu.PrefetchScalarGridSpec(num_...  26 us
    dot_general x4, matrix products, matmul(): return jnp.dot(left_side, right_side, preferred_element_type=F32)  24.6 us
    pallas_call x1, Pallas kernels, run_cross_forward(): pl.pallas_call(cross_forward, grid=(nseq, PAIRS), in_specs=[spec((length,...  20.4 us
  transfers between devices with their start and end apart: 5, of which 0 were waited for; matrix products, arithmetic and copies ran while one was open for 9% of the time, Pallas kernels for 57%

commit v1 on v0

--- a/solution.py
+++ b/solution.py
@@ -395,11 +395,28 @@
     )(query, kv, kv, upstream, context, lse)
 
 
-def run_self_backward(prefix, qkv, upstream, context, lse, bias, nseq):
+def run_self_backward(prefix, qkv, upstream, context, lse, bias, nseq, carried=None):
     length = qkv.shape[0] // nseq
     rows = spec((length, LANES), lambda p, s, _: (s, p))
+    group = []
+    kernel = self_backward
+    extra_out_specs = []
+    extra_out_shape = []
+    extra_scratch = []
+    params = None
+    if carried is not None:
+        group, collective_id = carried
+        shape = square_shape(group, LINE)
+        kernel = functools.partial(carried_backward, shape, LINE, PAIRS * nseq)
+        total = shape.total_shape(LINE)
+        extra_out_specs = [spec(total, lambda p, s, _: (0, 0, 0, 0))]
+        extra_out_shape = [jax.ShapeDtypeStruct(total, BF16)]
+        extra_scratch = shape.plane_scratch(LINE)
+        params = pltpu.CompilerParams(
+            collective_id=collective_id, has_side_effects=True, vmem_limit_bytes=60 << 20
+        )
     return pl.pallas_call(
-        self_backward,
+        kernel,
         grid_spec=pltpu.PrefetchScalarGridSpec(
             num_scalar_prefetch=1,
             grid=(PAIRS, nseq),
@@ -411,22 +428,26 @@
                 rows,
                 spec((None, None, 2, length), lambda p, s, _: (s, p, 0, 0)),
                 spec((2, LANES, 2 * length - LANES), lambda p, s, _: (p, 0, 0)),
-            ],
+            ]
+            + [pl.BlockSpec(memory_space=pl.ANY)] * len(group),
             out_specs=[
                 rows,
                 rows,
                 rows,
                 spec((None, 2, 2 * length), lambda p, s, _: (p, 0, 0)),
-            ],
-            scratch_shapes=[pltpu.VMEM((2, LANES, 2 * length - LANES), F32)],
+            ]
+            + extra_out_specs,
+            scratch_shapes=[pltpu.VMEM((2, LANES, 2 * length - LANES), F32)] + extra_scratch,
         ),
         out_shape=[jax.ShapeDtypeStruct(upstream.shape, BF16)] * 3
-        + [jax.ShapeDtypeStruct((PAIRS, 2, 2 * length), F32)],
+        + [jax.ShapeDtypeStruct((PAIRS, 2, 2 * length), F32)]
+        + extra_out_shape,
         cost_estimate=pl.CostEstimate(
             flops=24_000_000_000, bytes_accessed=20_000_000, transcendentals=0
         ),
+        compiler_params=params,
         name="self_backward",
-    )(prefix, qkv, qkv, qkv, upstream, context, lse, bias)
+    )(prefix, qkv, qkv, qkv, upstream, context, lse, bias, *group)
 
 
 FEED_BLOCK = 256
@@ -1015,39 +1036,50 @@
             return jax.ShapeDtypeStruct((4, self.part_rows, self.part_columns), F32)
         return jax.ShapeDtypeStruct((self.rows, self.block[1]), F32)
 
-    def scratch(self, line):
+    def total_shape(self, line):
+        return (line, 2) + self.block
+
+    def plane_scratch(self, line):
         rows, columns = self.block
         dma = pltpu.SemaphoreType.DMA
-        buffers = [
+        return [
             pltpu.VMEM((line, 8, rows, columns), BF16),
             pltpu.VMEM((line, 8, rows, columns), BF16),
             pltpu.VMEM((line, 2, 2, rows, columns), BF16),
             pltpu.VMEM((line, 2, rows, columns), BF16),
-            pltpu.VMEM((line, 2, rows, columns), BF16),
-            pltpu.VMEM((2, line, 2, rows, columns), BF16),
-            pltpu.VMEM((4, self.part_rows, self.part_columns), F32),
-            pltpu.VMEM((4, self.part_rows, self.part_columns), F32),
             dma((line,)),
             dma((2, line)),
             dma((2, line, 2)),
             dma((2, line, 2)),
+        ]
+
+    def line_scratch(self, line):
+        dma = pltpu.SemaphoreType.DMA
+        return [
+            pltpu.VMEM(self.total_shape(line), BF16),
+            pltpu.VMEM((2,) + self.total_shape(line), BF16),
+            pltpu.VMEM((4, self.part_rows, self.part_columns), F32),
+            pltpu.VMEM((4, self.part_rows, self.part_columns), F32),
+            dma((1,)),
             dma((2, 2, line)),
             dma((2, 3)),
         ]
-        return buffers
-
-
-REDUCE_SCRATCH = 14
+
+
+PLANE_SCRATCH = 8
+LINE_SCRATCH = 7
+
+
+def reduce_order(line):
+    return [line - 1, 0] + list(range(line - 2, 0, -1))
 
 
 def added(left, right):
     return (left.astype(F32) + right.astype(F32)).astype(BF16)
 
 
-def reduce_steps(place, shape, refs, out, scratch):
-    own, other, first_in, second_in, total, line_in, parts, gathered = scratch[:8]
-    load_sem, pair_sem, first_sem, second_sem, line_sem, swap_sem = scratch[8:]
-    line = place.line
+def plane_steps(place, shape, refs, total, scratch):
+    own, other, first_in, second_in, load_sem, pair_sem, first_sem, second_sem = scratch
     near = (place.x, place.y)
     far = (place.y, place.x)
     near_device = (place.at_x(), place.at_y())
@@ -1100,6 +1132,50 @@
             far_device[half],
         )
 
+    def pair_add(z):
+        pltpu.make_async_copy(own.at[z], own.at[z], load_sem.at[z]).wait()
+        pair_all(z).wait_recv()
+
+        @pl.loop(0, 8)
+        def _(slot):
+            own[z, slot] = added(own[z, slot], other[z, slot])
+
+        for half in range(2):
+            first(z, half).start()
+
+    def first_add(z):
+        for half in range(2):
+            first(z, half).wait_recv()
+            base = half * 4 + near[half] * 2
+
+            @pl.loop(0, 2)
+            def _(index):
+                own[z, base + index] = added(own[z, base + index], first_in[z, half, index])
+
+            second(z, half).start()
+
+    def second_add(z):
+        for half in range(2):
+            second(z, half).wait_recv()
+            mine = half * 4 + near[half] * 2 + far[half]
+            total[z, half] = added(own[z, mine], second_in[z, half])
+
+    def drain(z):
+        pair_all(z).wait_send()
+        for half in range(2):
+            first(z, half).wait_send()
+            second(z, half).wait_send()
+
+    return start, pair_add, first_add, second_add, drain
+
+
+def line_steps(place, shape, source, out, scratch):
+    total, line_in, parts, gathered, load_sem, line_sem, swap_sem = scratch
+    line = place.line
+
+    def load():
+        return pltpu.make_async_copy(source, total, load_sem.at[0])
+
     def along(z, side):
         return remote(
             total.at[z],
@@ -1108,34 +1184,6 @@
             line_sem.at[1, side, z],
             place.at_line(side),
         )
-
-    def pair_add(z):
-        pltpu.make_async_copy(own.at[z], own.at[z], load_sem.at[z]).wait()
-        pair_all(z).wait_recv()
-
-        @pl.loop(0, 8)
-        def _(slot):
-            own[z, slot] = added(own[z, slot], other[z, slot])
-
-        for half in range(2):
-            first(z, half).start()
-
-    def first_add(z):
-        for half in range(2):
-            first(z, half).wait_recv()
-            base = half * 4 + near[half] * 2
-
-            @pl.loop(0, 2)
-            def _(index):
-                own[z, base + index] = added(own[z, base + index], first_in[z, half, index])
-
-            second(z, half).start()
-
-    def second_add(z):
-        for half in range(2):
-            second(z, half).wait_recv()
-            mine = half * 4 + near[half] * 2 + far[half]
-            total[z, half] = added(own[z, mine], second_in[z, half])
 
     def line_send(z, side):
         ahead = place.z < z if side == 0 else place.z > z
@@ -1195,49 +1243,26 @@
                 copy.start()
             gathered[place.rep] = parts[place.rep]
 
+    def send(z):
+        line_send(z, 0)
+        line_send(z, 1)
+
+    def close():
+        for z in range(line):
+            line_end(z)
+        finish()
+
     def drain():
         if shape.exchange:
             for copy in swaps():
                 copy.wait()
             out[...] = gathered[...]
         for z in range(line):
-            pair_all(z).wait_send()
-            for half in range(2):
-                first(z, half).wait_send()
-                second(z, half).wait_send()
             for side in range(2):
                 ahead = place.z < z if side == 0 else place.z > z
                 pl.when(ahead)(lambda: along(z, side).wait_send())
 
-    order = [line - 1, 0] + [z for z in range(line - 2, 0, -1)]
-
-    def begin():
-        for z in order:
-            start(z)
-
-    def pairs():
-        for z in order:
-            pair_add(z)
-
-    def firsts():
-        for z in order:
-            first_add(z)
-
-    def seconds():
-        for index, z in enumerate(order):
-            second_add(z)
-            if index > 0:
-                line_send(order[index - 1], 0)
-                line_send(order[index - 1], 1)
-        line_send(order[-1], 0)
-        line_send(order[-1], 1)
-
-    def close():
-        for z in range(line):
-            line_end(z)
-        finish()
-
-    return begin, pairs, firsts, seconds, close, drain
+    return load, send, close, drain
 
 
 class VectorSum:
@@ -1288,88 +1313,116 @@
             self.copy(index).wait_send()
 
 
-def reduce_kernel(shapes, line, vector_count, *refs):
-    sources = []
-    at = 0
-    for shape in shapes:
-        sources.append(refs[at : at + shape.sources])
-        at += shape.sources
-    vector_refs = refs[at : at + vector_count]
-    at += vector_count
-    outs = refs[at : at + len(shapes)]
-    at += len(shapes)
-    vector_outs = refs[at : at + vector_count]
-    at += vector_count
+def carried_backward(shape, line, steps, *refs):
+    count = shape.sources
+    local, sources, outs = refs[:8], refs[8 : 8 + count], refs[8 + count : 12 + count]
+    total, acc_ref, *scratch = refs[12 + count :]
+    place = Place(line)
+    order = reduce_order(line)
+    start, pair_add, first_add, second_add, drain = plane_steps(
+        place, shape, sources, total, scratch
+    )
+    step = pl.program_id(0) * pl.num_programs(1) + pl.program_id(1)
+
+    @pl.when(step == 0)
+    def _():
+        place.greet()
+        for z in order:
+            start(z)
+
+    @pl.when(step == 1)
+    def _():
+        for z in order:
+            pair_add(z)
+
+    for index, z in enumerate(order):
+        pl.when(step == min(3 + 2 * index - index // 2, steps - 1))(
+            functools.partial(first_add, z)
+        )
+    self_backward(*local, *outs, acc_ref)
+
+    @pl.when(step == steps - 1)
+    def _():
+        for z in order:
+            second_add(z)
+        for z in order:
+            drain(z)
+
+
+def reduce_kernel(ready_shape, shape, line, *refs):
+    count = shape.sources
+    ready, sources, vector_ref = refs[0], refs[1 : 1 + count], refs[1 + count]
+    ready_out, out, vector_out = refs[2 + count : 5 + count]
+    scratch = refs[5 + count :]
+    ready_scratch, scratch = scratch[:LINE_SCRATCH], scratch[LINE_SCRATCH:]
+    line_scratch, scratch = scratch[:LINE_SCRATCH], scratch[LINE_SCRATCH:]
+    plane_scratch, scratch = scratch[:PLANE_SCRATCH], scratch[PLANE_SCRATCH:]
     place = Place(line)
     place.greet(wide=True)
-    plans = []
-    for index, shape in enumerate(shapes):
-        part = refs[at : at + REDUCE_SCRATCH]
-        at += REDUCE_SCRATCH
-        plans.append(reduce_steps(place, shape, sources[index], outs[index], part))
-    vectors = []
-    if vector_count:
-        vectors = [VectorSum(place, vector_refs[0], vector_outs[0], refs[at : at + 3])]
-
-    def rounds(*indices):
-        for vector in vectors:
-            for index in indices:
-                vector.round(index)
-
-    rounds(0)
-    for plan in plans:
-        plan[0]()
-    plans[0][1]()
-    rounds(1)
-    plans[0][2]()
-    rounds(2)
-    for index, plan in enumerate(plans):
-        ahead = plans[index + 1] if index + 1 < len(plans) else None
-        if ahead is not None:
-            ahead[1]()
-        plan[3]()
-        if ahead is not None:
-            ahead[2]()
-    rounds(3)
-    for plan in plans:
-        plan[4]()
-    rounds(4, 5)
-    for plan in plans:
-        plan[5]()
-    for vector in vectors:
-        vector.finish()
-
-
-def fast_reduce(groups, kinds, line, collective_id, vector=None):
-    shapes = []
-    blocks = []
-    scratch = []
-    for group, kind in zip(groups, kinds):
-        rows, columns = group[0].shape
-        shape = ReduceShape(kind, rows // (2 * line), columns, len(group))
-        shapes.append(shape)
-        blocks.extend(group)
-        scratch.extend(shape.scratch(line))
+    order = reduce_order(line)
+    start, pair_add, first_add, second_add, drain = plane_steps(
+        place, shape, sources, line_scratch[0], plane_scratch
+    )
+    ready_load, ready_send, ready_close, ready_drain = line_steps(
+        place, ready_shape, ready, ready_out, ready_scratch
+    )
+    _, send, close, line_drain = line_steps(place, shape, None, out, line_scratch)
+    vector = VectorSum(place, vector_ref, vector_out, scratch)
+    for z in order:
+        start(z)
+    ready_load().start()
+    vector.round(0)
+    for index, z in enumerate(order):
+        pair_add(z)
+        if index == 0:
+            ready_load().wait()
+    vector.round(1)
+    for index, z in enumerate(order):
+        ready_send(z)
+        first_add(z)
+        if index == 1:
+            vector.round(2)
+    ready_close()
+    vector.round(3)
+    for index, z in enumerate(order):
+        second_add(z)
+        if index > 0:
+            send(order[index - 1])
+    send(order[-1])
+    vector.round(4)
+    close()
+    vector.round(5)
+    ready_drain()
+    line_drain()
+    for z in order:
+        drain(z)
+    vector.finish()
+
+
+def square_shape(group, line):
+    rows, columns = group[0].shape
+    return ReduceShape("four", rows // (2 * line), columns, len(group))
+
+
+def fast_reduce(ready, group, line, collective_id, vector):
+    shape = square_shape(group, line)
     anywhere = pl.BlockSpec(memory_space=pl.ANY)
     local = pl.BlockSpec(memory_space=pltpu.VMEM)
-    in_specs = [anywhere] * len(blocks)
-    out_shape = [shape.out_shape() for shape in shapes]
-    if vector is not None:
-        blocks.append(vector)
-        in_specs.append(local)
-        out_shape.append(jax.ShapeDtypeStruct(vector.shape, F32))
-        scratch.extend(VectorSum.scratch(vector.shape))
+    out_shape = [shape.out_shape()] * 2 + [jax.ShapeDtypeStruct(vector.shape, F32)]
     return pl.pallas_call(
-        functools.partial(reduce_kernel, shapes, line, 0 if vector is None else 1),
-        in_specs=in_specs,
-        out_specs=[local] * len(out_shape),
+        functools.partial(reduce_kernel, shape, shape, line),
+        in_specs=[anywhere] * (1 + len(group)) + [local],
+        out_specs=[local] * 3,
         out_shape=out_shape,
-        scratch_shapes=scratch,
+        scratch_shapes=shape.line_scratch(line)
+        + shape.line_scratch(line)
+        + shape.plane_scratch(line)
+        + VectorSum.scratch(vector.shape),
         compiler_params=pltpu.CompilerParams(
             collective_id=collective_id, has_side_effects=True, vmem_limit_bytes=60 << 20
         ),
         name="fast_reduce",
-    )(*blocks)
+    )(ready, *group, vector)
 
 
 PLANE = 4
@@ -1415,11 +1468,9 @@
     return outs
 
 
-def scatter_last(groups, vector, collective_id):
-    if small_plane():
-        *outs, total = fast_reduce(
-            groups, ["four"] * len(groups), LINE, collective_id, vector
-        )
+def scatter_last(ready, groups, vector, collective_id):
+    if ready is not None:
+        *outs, total = fast_reduce(ready, groups[1], LINE, collective_id, vector)
         return [[out[index] for index in range(4)] for out in outs], total
     outs = [scatter_columns([scatter(item) for item in group]) for group in groups]
     return outs, lax.psum(vector, ("rep", "fsdp"))
@@ -1535,8 +1586,15 @@
         memory_rows, key_two_grad, value_two_grad, second, 2, 3
     )
     cross_terms = [query_term, key_term, value_term, out_term]
-    query_grad, key_grad, value_grad, diagonal = run_self_backward(
-        prefix_len, qkv, context_grad, context, lse_self, bias, nseq
+    query_grad, key_grad, value_grad, diagonal, *sums = run_self_backward(
+        prefix_len,
+        qkv,
+        context_grad,
+        context,
+        lse_self,
+        bias,
+        nseq,
+        (cross_terms, 2) if small_plane() else None,
     )
     tokens_grad, gain_first_grad, *self_terms = run_close(
         tokens.reshape(rows, width),
@@ -1580,7 +1638,7 @@
     gate_weight_grad = pair_grad[:, :, 0].reshape(shard, -1)
     up_weight_grad = pair_grad[:, :, 1].reshape(shard, -1)
     (cross_out_grads, self_out_grads), totals = scatter_last(
-        [cross_terms, self_terms], vector_block, 3
+        sums[0] if sums else None, [cross_terms, self_terms], vector_block, 3
     )
     own = lax.dynamic_slice(
         totals, (0, lax.axis_index("fsdp") * shard), (totals.shape[0], shard)

time: 409 us -> 397 us (0.971)
  Pallas kernels: 342 us -> 331 us
    pallas_call x2, Pallas kernels: 101 us -> 89.4 us  [the longest x1 56.3 us: fast_reduce(): pl.pallas_call(functools.partial(reduce_kernel, shape, shape, line), in_s...]
  transfers between devices with their start and end apart: 5 -> 5, of which waited for: 0 -> 0; matrix products, arithmetic and copies ran while one was open for 9% -> 9% of each run, Pallas kernels for 57% -> 56%
where the time goes in v1:
time: 397 us; the launch traced here: 394 us
  Pallas kernels  331 us (83%)
  matrix products  26.2 us (7%)
  local copies, waits for them, and re-layouts  15.8 us (4%)
  between operations  14.3 us (4%)
  other arithmetic  5.36 us (1%)
    pallas_call x1, Pallas kernels, fast_gather(): pl.pallas_call(functools.partial(gather_kernel, shapes, line), in_specs=[...  63.3 us
    pallas_call x1, Pallas kernels, fast_reduce(): pl.pallas_call(functools.partial(reduce_kernel, shape, shape, line), in_s...  56.3 us
    pallas_call x1, Pallas kernels, run_feed(): pl.pallas_call(feed_kernel, grid=(blocks,), in_specs=[whole(rows, **once)...  46.8 us
    pallas_call x1, Pallas kernels, run_cross_backward(): pl.pallas_call(cross_backward, grid=(nseq, PAIRS), in_specs=[rows, wide,...  36.3 us
    pallas_call x1, Pallas kernels, run_self_backward(): pl.pallas_call(kernel, grid_spec=pltpu.PrefetchScalarGridSpec(num_scalar_...  33.1 us
    pallas_call x2, Pallas kernels, run_close(): pl.pallas_call(functools.partial(close_kernel, count, project is not None...  32.4 us
    dot_general x4, matrix products, matmul(): return jnp.dot(left_side, right_side, preferred_element_type=F32)  24.5 us
    pallas_call x1, Pallas kernels, run_cross_forward(): pl.pallas_call(cross_forward, grid=(nseq, PAIRS), in_specs=[spec((length,...  20.5 us
  transfers between devices with their start and end apart: 5, of which 0 were waited for; matrix products, arithmetic and copies ran while one was open for 9% of the time, Pallas kernels for 56%

profile of v1, /device:TPU:0, one launch (start us, length us, event | category | flops | bytes accessed | tf_op | source)
XLA Modules:
  0.0 393.9 jit_solution(4659062597532697973)
XLA Ops:
  7.3 0.8 pad_bitcast_fusion
  8.0 0.7 pad_maximum_fusion.1
  8.8 0.6 pad.25.refs_3_.refs_9_
  9.5 2.0 pad_maximum_fusion
  11.5 63.3 %fast_gather.1 = (bf16[768,2560]{1,0:T(8,128)(2,1)}, bf16[768,4096]{1,0:T(8,128)(2,1)}, bf16[2048,768]{1,0:T(8,128)(2,1)}) custom-call(bf16[96,768]{1,0:T(8,128)(2,1)} %refs_0_.2, bf16[96,768]{1,0:T(8,128)(2,1)} %refs_1_.1, bf16[96,768]{1,0:T(8,128)(2,1)} %refs_2_.1, bf16[96,256]{1,0:T(8,128)(2,1)} %pad.25.refs_3_.refs_9_, bf16[96,768]{1,0:T(8,128)(2,1)} %refs_4_.1, ...), custom_call_target="tpu_custom_call" | custom-call | tf_op jit(solution)/shard_map/fast_gather/pallas_call | solution.py:994
  75.5 1.1 fusion.17
  78.2 4.9 %skewed_bias.1.bias_ref.refs_7_ = f32[12,128,896]{2,1,0:T(8,128)} custom-call(bf16[16,32]{1,0:T(8,128)(2,1)} %pad.26.table_ref, s32[1,1024]{1,0:T(1,128)} %bitcast.74), custom_call_target="tpu_custom_call" | custom-call | tf_op jit(solution)/shard_map/skewed_bias/pallas_call | solution.py:94
  83.7 7.6 %convolution_convert_fusion.1.query_ref.key_ref.value_ref.refs_1_.refs_2_.refs_3_ = bf16[1024,2304]{1,0:T(8,128)(2,1)} fusion(bf16[768,2560]{1,0:T(8,128)(2,1)} %get-tuple-element.78.refs_8_.refs_9_.refs_10_, bf16[1024,768]{1,0:T(8,128)(2,1)S(1)} %bitcast.66, f32[768]{0:T(1024)S(1)} %get-tuple-element.135, f32[1024]{0:T(1024)S(1)} %bitcast.77), kind=kOutput, calls=%fused_computation.2 | convolution fusion | flops 3629383680 | bytes 9837568 | tf_op jit(solution)/shard_map/dot_general | solution.py:28
  91.3 20.2 %self_forward.1 = (bf16[1024,768]{1,0:T(8,128)(2,1)}, f32[2,6,2,512]{3,2,1,0:T(2,128)}) custom-call(s32[2]{0:T(128)} %refs_0_.3, bf16[1024,2304]{1,0:T(8,128)(2,1)} %convolution_convert_fusion.1.query_ref.key_ref.value_ref.refs_1_.refs_2_.refs_3_, bf16[1024,2304]{1,0:T(8,128)(2,1)} %convolution_convert_fusion.1.query_ref.key_ref.value_ref.refs_1_.refs_2_.refs_3_, ...), custom_call_target="tpu_custom_call" | custom-call | flops 20000000000 | bytes 12000000 | tf_op jit(solution)/shard_map/self_forward/pallas_call | solution.py:316
  111.6 3.3 multiply_reduce_fusion
  114.9 5.0 %convolution_convert_fusion.2.query_ref = bf16[1024,768]{1,0:T(8,128)(2,1)} fusion(f32[1024,768]{1,0:T(8,128)S(1)} %get-tuple-element.151.middle_ref.refs_0_, f32[768]{0:T(1024)S(1)} %get-tuple-element.134, f32[1024]{0:T(1024)S(1)} %add_rsqrt_fusion, bf16[768,4096]{1,0:T(8,128)(2,1)} %get-tuple-element.80.out_proj_ref.refs_6_.refs_7_.key_ref.value_ref), kind=kOutput, calls=%fused_computation.12 | convolution fusion | flops 1211105280 | bytes 5905408 | tf_op jit(solution)/shard_map/dot_general | solution.py:28
  119.9 8.6 %fusion.key_ref.value_ref = bf16[2048,1536]{1,0:T(8,128)(2,1)} fusion(bf16[2048,768]{1,0:T(8,128)(2,1)S(1)} %bitcast.82, bf16[768,4096]{1,0:T(8,128)(2,1)} %get-tuple-element.80.out_proj_ref.refs_6_.refs_7_.key_ref.value_ref), kind=kOutput, calls=%fused_computation.1 | convolution fusion | flops 4834983936 | bytes 11796480 | tf_op jit(solution)/shard_map/dot_general | solution.py:28
  128.5 20.5 %cross_forward.1 = (bf16[1024,768]{1,0:T(8,128)(2,1)}, f32[2,6,2,512]{3,2,1,0:T(2,128)}) custom-call(bf16[1024,768]{1,0:T(8,128)(2,1)} %convolution_convert_fusion.2.query_ref, bf16[2048,1536]{1,0:T(8,128)(2,1)} %fusion.key_ref.value_ref, bf16[2048,1536]{1,0:T(8,128)(2,1)} %fusion.key_ref.value_ref), custom_call_target="tpu_custom_call" | custom-call | flops 24000000000 | bytes 10000000 | tf_op jit(solution)/shard_map/cross_forward/pallas_call | solution.py:346
  149.0 46.8 %feed.1 = (bf16[1024,768]{1,0:T(8,128)(2,1)}, f32[1024,768]{1,0:T(8,128)}, bf16[1024,768]{1,0:T(8,128)(2,1)}, bf16[1024,768]{1,0:T(8,128)(2,1)}, f32[1,768]{1,0:...) custom-call(f32[1024,768]{1,0:T(8,128)} %copy-done.8, ...), custom_call_target="tpu_custom_call" | custom-call | flops 32000000000 | bytes 40000000 | tf_op jit(solution)/shard_map/feed/pallas_call | solution.py:553
  195.8 0.7 reduce-scatter.11.cloned.1.call-update
  196.5 36.3 %cross_backward.1 = (bf16[1024,768]{1,0:T(8,128)(2,1)}, bf16[2048,768]{1,0:T(8,128)(2,1)}, bf16[2048,768]{1,0:T(8,128)(2,1)}) custom-call(bf16[1024,768]{1,0:T(8,128)(2,1)} %convolution_convert_fusion.2.query_ref, bf16[2048,1536]{1,0:T(8,128)(2,1)} %fusion.key_ref.value_ref, bf16[2048,1536]{1,0:T(8,128)(2,1)} %fusion.key_ref.value_ref, ...), custom_call_target="tpu_custom_call" | custom-call | flops 35999997952 | bytes 20000000 | tf_op jit(solution)/shard_map/cross_backward/pallas_call | solution.py:374
  232.9 13.5 %cross_close.1 = (f32[1024,768]{1,0:T(8,128)}, f32[1,768]{1,0:T(1,128)}, bf16[768,768]{1,0:T(8,128)(2,1)}, bf16[768,768]{1,0:T(8,128)(2,1)}, bf16[1024,768]{1,0:T(8,128)(2,1)}, /*index=5*/bf16[1024,768]{1,0:T(8,128)(2,1)}) custom-call(f32[1024,768]{1,0:T(8,128)} %copy-done.8, f32[1024,768]{1,0:T(8,128)} %get-tuple-element.85.refs_1_, ...), custom_call_target="tpu_custom_call" | custom-call | flops 8000000000 | bytes 25000000 | tf_op jit(solution)/shard_map/cross_close/pallas_call | solution.py:667
  246.4 16.7 %memory_close.1 = (f32[2048,768]{1,0:T(8,128)}, bf16[768,768]{1,0:T(8,128)(2,1)}, bf16[768,768]{1,0:T(8,128)(2,1)}) custom-call(bf16[2048,768]{1,0:T(8,128)(2,1)} %bitcast.81, bf16[2048,768]{1,0:T(8,128)(2,1)} %get-tuple-element.95.key_grad_ref, bf16[2048,768]{1,0:T(8,128)(2,1)} %get-tuple-element.96.value_grad_ref, ...), custom_call_target="tpu_custom_call" | custom-call | flops 10000000000 | bytes 18000000 | tf_op jit(solution)/shard_map/memory_close/pallas_call | solution.py:719
  263.1 33.1 %self_backward.1 = (bf16[1024,768]{1,0:T(8,128)(2,1)}, bf16[1024,768]{1,0:T(8,128)(2,1)}, bf16[1024,768]{1,0:T(8,128)(2,1)}, f32[6,2,1024]{2,1,0:T(2,128)}, bf16[4,2,48,768]{3,2,1,0:T(8,128)(2,1)}) custom-call(s32[2]{0:T(128)} %refs_0_.3, bf16[1024,2304]{1,0:T(8,128)(2,1)} %convolution_convert_fusion.1.query_ref.key_ref.value_ref.refs_1_.refs_2_.refs_3_, ...), custom_call_target="tpu_custom_call" | custom-call | flops 24000000000 | bytes 20000000 | tf_op jit(solution)/shard_map/self_backward/pallas_call | solution.py:418
  296.2 18.9 %self_close.1 = (f32[1024,768]{1,0:T(8,128)}, f32[1,768]{1,0:T(1,128)}, bf16[768,768]{1,0:T(8,128)(2,1)}, bf16[768,768]{1,0:T(8,128)(2,1)}, bf16[768,768]{1,0:T(8,128)(2,1)}, /*index=5*/bf16[768,768]{1,0:T(8,128)(2,1)}) custom-call(bf16[1024,768]{1,0:T(8,128)(2,1)} %bitcast.65, f32[1024,768]{1,0:T(8,128)} %get-tuple-element.90.refs_1_, ...), custom_call_target="tpu_custom_call" | custom-call | flops 8000000000 | bytes 25000000 | tf_op jit(solution)/shard_map/self_close/pallas_call | solution.py:667
  315.2 2.1 copy.68
  317.3 1.9 copy.59
  319.9 0.6 fusion.12
  320.8 0.6 select_maximum_fusion.refs_5_
  321.4 56.3 %fast_reduce.1 = (f32[4,96,192]{2,1,0:T(8,128)}, f32[4,96,192]{2,1,0:T(8,128)}, f32[8,768]{1,0:T(8,128)}) custom-call(bf16[4,2,48,768]{3,2,1,0:T(8,128)(2,1)} %get-tuple-element.112.refs_0_, bf16[768,768]{1,0:T(8,128)(2,1)} %get-tuple-element.119.refs_1_, bf16[768,768]{1,0:T(8,128)(2,1)} %get-tuple-element.120.refs_2_, ...), custom_call_target="tpu_custom_call" | custom-call | tf_op jit(solution)/shard_map/fast_reduce/pallas_call | solution.py:1412
  377.7 0.8 constant_dynamic-slice_fusion
  379.5 2.1 slice_bitcast_fusion
  381.6 1.6 bitcast_convert_fusion
  383.2 1.3 reshape.126
  384.5 1.2 slice_reduce_fusion
  385.7 0.7 copy.65
  386.4 0.7 copy.66
  (52 shorter events, 5.0 us)
Async XLA Ops:
  7.2 67.9 %copy-start = (bf16[2,512,768]{2,1,0:T(8,128)(2,1)S(1)}, bf16[2,512,768]{2,1,0:T(8,128)(2,1)}, u32[]{:S(2)}) copy-start(bf16[2,512,768]{2,1,0:T(8,128)(2,1)} %param.20) | copy-start | bytes 4718596
  7.2 70.2 %copy-start.3 = (s32[1023]{0:T(1024)S(1)}, s32[1023]{0:T(1024)}, u32[]{:S(2)}) copy-start(s32[1023]{0:T(1024)} %param.23) | copy-start | bytes 12280
  7.2 141.7 %all-gather.2.cloned.1.call-start = ((), (), s32[]{:S(2)}) async-start(), calls=%async_computation.4 | async-start | bytes 7077888 | tf_op jit(solution)/shard_map/all_gather | solution.py:1438
  74.9 240.3 %reduce-scatter.9.cloned.1.call-start = ((), (), s32[]{:S(2)}) async-start(), calls=%async_computation.5 | async-start | bytes 3538944 | tf_op jit(solution)/shard_map/reduce_scatter | solution.py:1448
  114.9 5.0 %copy-start.8 = (f32[1024,768]{1,0:T(8,128)}, f32[1024,768]{1,0:T(8,128)S(1)}, u32[]{:S(2)}) copy-start(f32[1024,768]{1,0:T(8,128)S(1)} %get-tuple-element.151.middle_ref.refs_0_) | copy-start | bytes 9437188
  114.9 5.0 %copy-start.7 = (bf16[2,1024,768]{2,1,0:T(8,128)(2,1)S(1)}, bf16[2,1024,768]{2,1,0:T(8,128)(2,1)}, u32[]{:S(2)}) copy-start(bf16[2,1024,768]{2,1,0:T(8,128)(2,1)} %param.21) | copy-start | bytes 9437188
  195.7 119.5 %reduce-scatter.11.cloned.1.call-start = ((), (), s32[]{:S(2)}) async-start(), calls=%async_computation.6 | async-start | bytes 7077888 | tf_op jit(solution)/shard_map/reduce_scatter | solution.py:1448
  196.5 185.2 %reduce-scatter.15.cloned.1.call-start = ((), (), s32[]{:S(2)}) async-start(), calls=%async_computation.8 | async-start | bytes 491520
  315.1 4.8 %copy-start.1 = (f32[6,2,1024]{2,1,0:T(2,128)S(1)}, f32[6,2,1024]{2,1,0:T(2,128)}, u32[]{:S(2)}) copy-start(f32[6,2,1024]{2,1,0:T(2,128)} %get-tuple-element.126) | copy-start | bytes 147460
  315.1 4.8 %copy-start.2 = (s32[1024]{0:T(1024)S(1)}, s32[1024]{0:T(1024)}, u32[]{:S(2)}) copy-start(s32[1024]{0:T(1024)} %pad.27) | copy-start | bytes 12292
  315.1 5.6 %copy-start.4 = (f32[1,768]{1,0:T(1,128)S(1)}, f32[1,768]{1,0:T(1,128)}, u32[]{:S(2)}) copy-start(f32[1,768]{1,0:T(1,128)} %get-tuple-element.125) | copy-start | bytes 9220
  315.1 5.6 %copy-start.5 = (f32[1,768]{1,0:T(1,128)S(1)}, f32[1,768]{1,0:T(1,128)}, u32[]{:S(2)}) copy-start(f32[1,768]{1,0:T(1,128)} %get-tuple-element.124) | copy-start | bytes 9220
  315.2 5.6 %copy-start.6 = (f32[1,768]{1,0:T(1,128)S(1)}, f32[1,768]{1,0:T(1,128)}, u32[]{:S(2)}) copy-start(f32[1,768]{1,0:T(1,128)} %get-tuple-element.123) | copy-start | bytes 9220
  319.3 63.9 %reduce-scatter.13.cloned.1.call-start = ((), (), s32[]{:S(2)}) async-start(), calls=%async_computation.7 | async-start | bytes 983040
Sparse Core Ops, SparseCore 0:
  75.0 62.7 all-gather.1
  195.9 38.7 reduce-scatter.8
  237.0 69.0 reduce-scatter.10
  319.4 24.7 reduce-scatter.14
  346.9 27.2 reduce-scatter.12

commit v2 on v1

--- a/solution.py
+++ b/solution.py
@@ -366,13 +366,38 @@
     )(query, kv, kv)
 
 
-def run_cross_backward(query, kv, upstream, context, lse, nseq):
+def carry(carried, steps, inner, inputs, outputs):
+    if carried is None:
+        return inner, [], [], [], [], None
+    group, kind, collective_id = carried
+    shape = group_shape(group, kind, LINE)
+    kernel = functools.partial(
+        carried_kernel, shape, LINE, steps, inner, inputs, outputs
+    )
+    total = shape.total_shape(LINE)
+    params = pltpu.CompilerParams(
+        collective_id=collective_id, has_side_effects=True, vmem_limit_bytes=60 << 20
+    )
+    return (
+        kernel,
+        group,
+        [pl.BlockSpec(total, lambda *_: (0, 0, 0, 0))],
+        [jax.ShapeDtypeStruct(total, BF16)],
+        shape.plane_scratch(LINE),
+        params,
+    )
+
+
+def run_cross_backward(query, kv, upstream, context, lse, nseq, carried=None):
     length = query.shape[0] // nseq
     count = kv.shape[0] // nseq
     rows = spec((length, LANES), lambda s, p: (s, p))
     wide = spec((count, LANES), lambda s, p: (s, p))
+    kernel, group, total_specs, totals, scratch, params = carry(
+        carried, PAIRS * nseq, cross_backward, 6, 3
+    )
     return pl.pallas_call(
-        cross_backward,
+        kernel,
         grid=(nseq, PAIRS),
         in_specs=[
             rows,
@@ -381,40 +406,30 @@
             rows,
             rows,
             spec((None, None, 2, length), lambda s, p: (s, p, 0, 0)),
-        ],
-        out_specs=[rows, wide, wide],
+        ]
+        + [pl.BlockSpec(memory_space=pl.ANY)] * len(group),
+        out_specs=[rows, wide, wide] + total_specs,
         out_shape=[
             jax.ShapeDtypeStruct(query.shape, BF16),
             jax.ShapeDtypeStruct((kv.shape[0], PAIRS * LANES), BF16),
             jax.ShapeDtypeStruct((kv.shape[0], PAIRS * LANES), BF16),
-        ],
+        ]
+        + totals,
+        scratch_shapes=scratch,
         cost_estimate=pl.CostEstimate(
             flops=36_000_000_000, bytes_accessed=20_000_000, transcendentals=0
         ),
+        compiler_params=params,
         name="cross_backward",
-    )(query, kv, kv, upstream, context, lse)
+    )(query, kv, kv, upstream, context, lse, *group)
 
 
 def run_self_backward(prefix, qkv, upstream, context, lse, bias, nseq, carried=None):
     length = qkv.shape[0] // nseq
     rows = spec((length, LANES), lambda p, s, _: (s, p))
-    group = []
-    kernel = self_backward
-    extra_out_specs = []
-    extra_out_shape = []
-    extra_scratch = []
-    params = None
-    if carried is not None:
-        group, collective_id = carried
-        shape = square_shape(group, LINE)
-        kernel = functools.partial(carried_backward, shape, LINE, PAIRS * nseq)
-        total = shape.total_shape(LINE)
-        extra_out_specs = [spec(total, lambda p, s, _: (0, 0, 0, 0))]
-        extra_out_shape = [jax.ShapeDtypeStruct(total, BF16)]
-        extra_scratch = shape.plane_scratch(LINE)
-        params = pltpu.CompilerParams(
-            collective_id=collective_id, has_side_effects=True, vmem_limit_bytes=60 << 20
-        )
+    kernel, group, total_specs, totals, scratch, params = carry(
+        carried, PAIRS * nseq, self_backward, 8, 4
+    )
     return pl.pallas_call(
         kernel,
         grid_spec=pltpu.PrefetchScalarGridSpec(
@@ -436,12 +451,12 @@
                 rows,
                 spec((None, 2, 2 * length), lambda p, s, _: (p, 0, 0)),
             ]
-            + extra_out_specs,
-            scratch_shapes=[pltpu.VMEM((2, LANES, 2 * length - LANES), F32)] + extra_scratch,
+            + total_specs,
+            scratch_shapes=[pltpu.VMEM((2, LANES, 2 * length - LANES), F32)] + scratch,
         ),
         out_shape=[jax.ShapeDtypeStruct(upstream.shape, BF16)] * 3
         + [jax.ShapeDtypeStruct((PAIRS, 2, 2 * length), F32)]
-        + extra_out_shape,
+        + totals,
         cost_estimate=pl.CostEstimate(
             flops=24_000_000_000, bytes_accessed=20_000_000, transcendentals=0
         ),
@@ -911,10 +926,9 @@
         )
 
     def each(fn):
-        def run():
-            for hop in range(hops):
-                for side in range(2):
-                    pl.when(place.arrives(side, hop))(functools.partial(fn, side, hop))
+        def run(hop):
+            for side in range(2):
+                pl.when(place.arrives(side, hop))(functools.partial(fn, side, hop))
 
         return run
 
@@ -954,7 +968,8 @@
             if hop + 1 < hops:
                 pl.when(place.has_next(side))(lambda: line_next(side, hop + 1).wait_send())
 
-        each(last)()
+        for hop in range(hops):
+            each(last)(hop)
         for side in range(2):
             pl.when(place.has_next(side))(lambda side=side: line_first(side).wait_send())
         own_pair().wait()
@@ -978,9 +993,16 @@
     for index, shape in enumerate(shapes):
         own, *sems = scratch[4 * index : 4 * index + 4]
         plans.append(gather_steps(place, shape, sources[index], own, targets[index], sems))
-    for stage in range(5):
-        for plan in plans:
-            plan[stage]()
+    for plan in plans:
+        plan[0]()
+    for step in range(line + 1):
+        for stage in range(3):
+            hop = step - stage
+            if 0 <= hop < line - 1:
+                for plan in plans:
+                    plan[1 + stage](hop)
+    for plan in plans:
+        plan[4]()
 
 
 def fast_gather(groups, line, by_rows, collective_id):
@@ -1313,14 +1335,16 @@
             self.copy(index).wait_send()
 
 
-def carried_backward(shape, line, steps, *refs):
-    count = shape.sources
-    local, sources, outs = refs[:8], refs[8 : 8 + count], refs[8 + count : 12 + count]
-    total, acc_ref, *scratch = refs[12 + count :]
+def carried_kernel(shape, line, steps, inner, inputs, outputs, *refs):
+    split = inputs + shape.sources
+    local, sources = refs[:inputs], refs[inputs:split]
+    outs = refs[split : split + outputs]
+    total = refs[split + outputs]
+    own = len(refs) - PLANE_SCRATCH
     place = Place(line)
     order = reduce_order(line)
     start, pair_add, first_add, second_add, drain = plane_steps(
-        place, shape, sources, total, scratch
+        place, shape, sources, total, refs[own:]
     )
     step = pl.program_id(0) * pl.num_programs(1) + pl.program_id(1)
 
@@ -1339,7 +1363,7 @@
         pl.when(step == min(3 + 2 * index - index // 2, steps - 1))(
             functools.partial(first_add, z)
         )
-    self_backward(*local, *outs, acc_ref)
+    inner(*local, *outs, *refs[split + outputs + 1 : own])
 
     @pl.when(step == steps - 1)
     def _():
@@ -1349,40 +1373,46 @@
             drain(z)
 
 
-def reduce_kernel(ready_shape, shape, line, *refs):
+def reduce_kernel(ready_shapes, shape, line, *refs):
     count = shape.sources
-    ready, sources, vector_ref = refs[0], refs[1 : 1 + count], refs[1 + count]
-    ready_out, out, vector_out = refs[2 + count : 5 + count]
-    scratch = refs[5 + count :]
-    ready_scratch, scratch = scratch[:LINE_SCRATCH], scratch[LINE_SCRATCH:]
-    line_scratch, scratch = scratch[:LINE_SCRATCH], scratch[LINE_SCRATCH:]
-    plane_scratch, scratch = scratch[:PLANE_SCRATCH], scratch[PLANE_SCRATCH:]
+    many = len(ready_shapes)
+    ready, sources = refs[:many], refs[many : many + count]
+    vector_ref = refs[many + count]
+    at = many + count + 1
+    ready_outs, out, vector_out = refs[at : at + many], refs[at + many], refs[at + many + 1]
+    scratch = refs[at + many + 2 :]
     place = Place(line)
     place.greet(wide=True)
     order = reduce_order(line)
+    plans = []
+    for index, ready_shape in enumerate(ready_shapes):
+        own, scratch = scratch[:LINE_SCRATCH], scratch[LINE_SCRATCH:]
+        plans.append(line_steps(place, ready_shape, ready[index], ready_outs[index], own))
+    line_scratch, scratch = scratch[:LINE_SCRATCH], scratch[LINE_SCRATCH:]
+    plane_scratch, scratch = scratch[:PLANE_SCRATCH], scratch[PLANE_SCRATCH:]
     start, pair_add, first_add, second_add, drain = plane_steps(
         place, shape, sources, line_scratch[0], plane_scratch
-    )
-    ready_load, ready_send, ready_close, ready_drain = line_steps(
-        place, ready_shape, ready, ready_out, ready_scratch
     )
     _, send, close, line_drain = line_steps(place, shape, None, out, line_scratch)
     vector = VectorSum(place, vector_ref, vector_out, scratch)
     for z in order:
         start(z)
-    ready_load().start()
+    for load, *_ in plans:
+        load().start()
     vector.round(0)
     for index, z in enumerate(order):
         pair_add(z)
-        if index == 0:
-            ready_load().wait()
+    for load, *_ in plans:
+        load().wait()
     vector.round(1)
     for index, z in enumerate(order):
-        ready_send(z)
+        for _, ready_send, _, _ in plans:
+            ready_send(z)
         first_add(z)
         if index == 1:
             vector.round(2)
-    ready_close()
+    for _, _, ready_close, _ in plans:
+        ready_close()
     vector.round(3)
     for index, z in enumerate(order):
         second_add(z)
@@ -1392,37 +1422,41 @@
     vector.round(4)
     close()
     vector.round(5)
-    ready_drain()
+    for _, _, _, ready_drain in plans:
+        ready_drain()
     line_drain()
     for z in order:
         drain(z)
     vector.finish()
 
 
-def square_shape(group, line):
+def group_shape(group, kind, line):
     rows, columns = group[0].shape
-    return ReduceShape("four", rows // (2 * line), columns, len(group))
-
-
-def fast_reduce(ready, group, line, collective_id, vector):
-    shape = square_shape(group, line)
+    return ReduceShape(kind, rows // (2 * line), columns, len(group))
+
+
+def fast_reduce(ready, ready_shapes, group, line, collective_id, vector):
+    shape = group_shape(group, "four", line)
     anywhere = pl.BlockSpec(memory_space=pl.ANY)
     local = pl.BlockSpec(memory_space=pltpu.VMEM)
-    out_shape = [shape.out_shape()] * 2 + [jax.ShapeDtypeStruct(vector.shape, F32)]
+    shapes = ready_shapes + [shape]
+    scratch = []
+    for item in shapes:
+        scratch.extend(item.line_scratch(line))
     return pl.pallas_call(
-        functools.partial(reduce_kernel, shape, shape, line),
-        in_specs=[anywhere] * (1 + len(group)) + [local],
-        out_specs=[local] * 3,
-        out_shape=out_shape,
-        scratch_shapes=shape.line_scratch(line)
-        + shape.line_scratch(line)
+        functools.partial(reduce_kernel, ready_shapes, shape, line),
+        in_specs=[anywhere] * (len(ready) + len(group)) + [local],
+        out_specs=[local] * (len(shapes) + 1),
+        out_shape=[item.out_shape() for item in shapes]
+        + [jax.ShapeDtypeStruct(vector.shape, F32)],
+        scratch_shapes=scratch
         + shape.plane_scratch(line)
         + VectorSum.scratch(vector.shape),
         compiler_params=pltpu.CompilerParams(
             collective_id=collective_id, has_side_effects=True, vmem_limit_bytes=60 << 20
         ),
         name="fast_reduce",
-    )(ready, *group, vector)
+    )(*ready, *group, vector)
 
 
 PLANE = 4
@@ -1468,12 +1502,22 @@
     return outs
 
 
-def scatter_last(ready, groups, vector, collective_id):
-    if ready is not None:
-        *outs, total = fast_reduce(ready, groups[1], LINE, collective_id, vector)
-        return [[out[index] for index in range(4)] for out in outs], total
-    outs = [scatter_columns([scatter(item) for item in group]) for group in groups]
-    return outs, lax.psum(vector, ("rep", "fsdp"))
+def scatter_last(down, cross, group, vector, collective_id):
+    down_term, down_sums = down
+    cross_group, cross_sums = cross
+    if small_plane():
+        shapes = [
+            group_shape(cross_group, "four", LINE),
+            group_shape([down_term], "rows", LINE),
+        ]
+        cross_out, down_out, group_out, total = fast_reduce(
+            [cross_sums[0], down_sums[0]], shapes, group, LINE, collective_id, vector
+        )
+        outs = [[out[index] for index in range(4)] for out in (cross_out, group_out)]
+        return down_out.reshape(-1, down_out.shape[2]), outs, total
+    (down_out,) = scatter_columns([scatter(down_term)])
+    outs = [scatter_columns([scatter(item) for item in part]) for part in (cross_group, group)]
+    return down_out, outs, lax.psum(vector, ("rep", "fsdp"))
 
 
 def body(
@@ -1559,10 +1603,16 @@
         down_term,
         pair_term,
     ) = run_feed(middle, context_two, second, 4, gain_third, upstream, gate_up, down)
-    down_own = scatter(down_term)
+    carries = small_plane()
     pair_own = scatter(pair_term)
-    query_two_grad, key_two_grad, value_two_grad = run_cross_backward(
-        query_two, kv_two, context_two_grad, context_two, lse_cross, nseq
+    query_two_grad, key_two_grad, value_two_grad, *down_sums = run_cross_backward(
+        query_two,
+        kv_two,
+        context_two_grad,
+        context_two,
+        lse_cross,
+        nseq,
+        ([down_term], "rows", 4) if carries else None,
     )
     (
         middle_grad,
@@ -1586,7 +1636,7 @@
         memory_rows, key_two_grad, value_two_grad, second, 2, 3
     )
     cross_terms = [query_term, key_term, value_term, out_term]
-    query_grad, key_grad, value_grad, diagonal, *sums = run_self_backward(
+    query_grad, key_grad, value_grad, diagonal, *cross_sums = run_self_backward(
         prefix_len,
         qkv,
         context_grad,
@@ -1594,8 +1644,9 @@
         lse_self,
         bias,
         nseq,
-        (cross_terms, 2) if small_plane() else None,
-    )
+        (cross_terms, "four", 2) if carries else None,
+    )
+    pair_split, query_grad = lax.optimization_barrier((column_blocks(pair_own), query_grad))
     tokens_grad, gain_first_grad, *self_terms = run_close(
         tokens.reshape(rows, width),
         middle_grad,
@@ -1624,21 +1675,12 @@
         ),
         ((0, 4), (0, 0)),
     )
-    down_own, pair_own, memory_grad, self_terms = lax.optimization_barrier(
-        (down_own, pair_own, memory_grad, self_terms)
-    )
-    down_split = column_blocks(down_own)
-    pair_split = column_blocks(pair_own)
-    down_split, pair_split, self_terms = lax.optimization_barrier(
-        (down_split, pair_split, self_terms)
-    )
-    down_weight_grad = lax.psum_scatter(down_split, "rep").astype(F32)
     pair_grad = lax.psum_scatter(pair_split, "rep").astype(F32)
     pair_grad = pair_grad.reshape(shard, -1, 2, FEED_BLOCK)
     gate_weight_grad = pair_grad[:, :, 0].reshape(shard, -1)
     up_weight_grad = pair_grad[:, :, 1].reshape(shard, -1)
-    (cross_out_grads, self_out_grads), totals = scatter_last(
-        sums[0] if sums else None, [cross_terms, self_terms], vector_block, 3
+    down_weight_grad, (cross_out_grads, self_out_grads), totals = scatter_last(
+        (down_term, down_sums), (cross_terms, cross_sums), self_terms, vector_block, 3
     )
     own = lax.dynamic_slice(
         totals, (0, lax.axis_index("fsdp") * shard), (totals.shape[0], shard)

time: 397 us -> 395 us (level)
    pallas_call x2, Pallas kernels: 92.7 us -> 99.2 us  [the longest x1 58.3 us: fast_reduce(): pl.pallas_call(functools.partial(reduce_kernel, ready_shapes, shape, line...]
    pallas_call x1, Pallas kernels: 63.3 us -> 56.9 us  [fast_gather(): pl.pallas_call(functools.partial(gather_kernel, shapes, line), in_specs=[...]
  transfers between devices with their start and end apart: 5 -> 3, of which waited for: 0 -> 0; matrix products, arithmetic and copies ran while one was open for 9% -> 9% of each run, Pallas kernels for 56% -> 58%
where the time goes in v2:
time: 395 us; the launch traced here: 391 us
  Pallas kernels  330 us (84%)
  matrix products  26.1 us (7%)
  local copies, waits for them, and re-layouts  16.4 us (4%)
  between operations  14.2 us (4%)
  other arithmetic  4.46 us (1%)
    pallas_call x1, Pallas kernels, fast_reduce(): pl.pallas_call(functools.partial(reduce_kernel, ready_shapes, shape, line...  58.3 us
    pallas_call x1, Pallas kernels, fast_gather(): pl.pallas_call(functools.partial(gather_kernel, shapes, line), in_specs=[...  56.9 us
    pallas_call x1, Pallas kernels, run_feed(): pl.pallas_call(feed_kernel, grid=(blocks,), in_specs=[whole(rows, **once)...  46.8 us
    pallas_call x1, Pallas kernels, run_cross_backward(): pl.pallas_call(kernel, grid=(nseq, PAIRS), in_specs=[rows, wide, spec((co...  40.9 us
    pallas_call x2, Pallas kernels, run_close(): pl.pallas_call(functools.partial(close_kernel, count, project is not None...  32.4 us
    pallas_call x1, Pallas kernels, run_self_backward(): pl.pallas_call(kernel, grid_spec=pltpu.PrefetchScalarGridSpec(num_scalar_...  31.9 us
    dot_general x4, matrix products, matmul(): return jnp.dot(left_side, right_side, preferred_element_type=F32)  24.4 us
    pallas_call x1, Pallas kernels, run_cross_forward(): pl.pallas_call(cross_forward, grid=(nseq, PAIRS), in_specs=[spec((length,...  20.4 us
  transfers between devices with their start and end apart: 3, of which 0 were waited for; matrix products, arithmetic and copies ran while one was open for 9% of the time, Pallas kernels for 58%

profile of v2, /device:TPU:0, one launch (start us, length us, event | category | flops | bytes accessed | tf_op | source)
XLA Modules:
  0.0 391.1 jit_solution(10394755027220373311)
XLA Ops:
  7.3 0.8 pad_bitcast_fusion
  8.0 0.7 pad_maximum_fusion.1
  8.8 0.6 pad.25.refs_3_.refs_9_
  9.5 2.0 pad_maximum_fusion
  11.5 56.9 %fast_gather.1 = (bf16[768,2560]{1,0:T(8,128)(2,1)}, bf16[768,4096]{1,0:T(8,128)(2,1)}, bf16[2048,768]{1,0:T(8,128)(2,1)}) custom-call(bf16[96,768]{1,0:T(8,128)(2,1)} %refs_0_.2, bf16[96,768]{1,0:T(8,128)(2,1)} %refs_1_.1, bf16[96,768]{1,0:T(8,128)(2,1)} %refs_2_.1, bf16[96,256]{1,0:T(8,128)(2,1)} %pad.25.refs_3_.refs_9_, bf16[96,768]{1,0:T(8,128)(2,1)} %refs_4_.1, ...), custom_call_target="tpu_custom_call" | custom-call | tf_op jit(solution)/shard_map/fast_gather/pallas_call | solution.py:1016
  69.1 1.1 fusion.17
  70.4 0.6 pad.26.table_ref
  71.8 5.1 %skewed_bias.1.bias_ref.refs_7_ = f32[12,128,896]{2,1,0:T(8,128)} custom-call(bf16[16,32]{1,0:T(8,128)(2,1)} %pad.26.table_ref, s32[1,1024]{1,0:T(1,128)} %bitcast.69), custom_call_target="tpu_custom_call" | custom-call | tf_op jit(solution)/shard_map/skewed_bias/pallas_call | solution.py:94
  77.4 7.6 %convolution_convert_fusion.1.query_ref.key_ref.value_ref.refs_1_.refs_2_.refs_3_ = bf16[1024,2304]{1,0:T(8,128)(2,1)} fusion(bf16[768,2560]{1,0:T(8,128)(2,1)} %get-tuple-element.69.refs_8_.refs_9_.refs_10_, bf16[1024,768]{1,0:T(8,128)(2,1)S(1)} %bitcast.61, f32[768]{0:T(1024)S(1)} %get-tuple-element.153, f32[1024]{0:T(1024)S(1)} %bitcast.72), kind=kOutput, calls=%fused_computation.2 | convolution fusion | flops 3629383680 | bytes 9837568 | tf_op jit(solution)/shard_map/dot_general | solution.py:28
  85.1 20.2 %self_forward.1 = (bf16[1024,768]{1,0:T(8,128)(2,1)}, f32[2,6,2,512]{3,2,1,0:T(2,128)}) custom-call(s32[2]{0:T(128)} %refs_0_.3, bf16[1024,2304]{1,0:T(8,128)(2,1)} %convolution_convert_fusion.1.query_ref.key_ref.value_ref.refs_1_.refs_2_.refs_3_, bf16[1024,2304]{1,0:T(8,128)(2,1)} %convolution_convert_fusion.1.query_ref.key_ref.value_ref.refs_1_.refs_2_.refs_3_, ...), custom_call_target="tpu_custom_call" | custom-call | flops 20000000000 | bytes 12000000 | tf_op jit(solution)/shard_map/self_forward/pallas_call | solution.py:316
  105.3 3.3 multiply_reduce_fusion
  108.6 5.0 %convolution_convert_fusion.2.query_ref.refs_0_ = bf16[1024,768]{1,0:T(8,128)(2,1)} fusion(f32[1024,768]{1,0:T(8,128)S(1)} %get-tuple-element.169.middle_ref.refs_0_, f32[768]{0:T(1024)S(1)} %get-tuple-element.152, f32[1024]{0:T(1024)S(1)} %add_rsqrt_fusion, bf16[768,4096]{1,0:T(8,128)(2,1)} %get-tuple-element.71.out_proj_ref.refs_6_.refs_7_.key_ref.value_ref), kind=kOutput, calls=%fused_computation.12 | convolution fusion | flops 1211105280 | bytes 5905408 | tf_op jit(solution)/shard_map/dot_general | solution.py:28
  113.6 8.5 %fusion.key_ref.value_ref.refs_1_.refs_2_ = bf16[2048,1536]{1,0:T(8,128)(2,1)} fusion(bf16[2048,768]{1,0:T(8,128)(2,1)S(1)} %bitcast.77, bf16[768,4096]{1,0:T(8,128)(2,1)} %get-tuple-element.71.out_proj_ref.refs_6_.refs_7_.key_ref.value_ref), kind=kOutput, calls=%fused_computation.1 | convolution fusion | flops 4834983936 | bytes 11796480 | tf_op jit(solution)/shard_map/dot_general | solution.py:28
  122.1 20.4 %cross_forward.1 = (bf16[1024,768]{1,0:T(8,128)(2,1)}, f32[2,6,2,512]{3,2,1,0:T(2,128)}) custom-call(bf16[1024,768]{1,0:T(8,128)(2,1)} %convolution_convert_fusion.2.query_ref.refs_0_, bf16[2048,1536]{1,0:T(8,128)(2,1)} %fusion.key_ref.value_ref.refs_1_.refs_2_, bf16[2048,1536]{1,0:T(8,128)(2,1)} %fusion.key_ref.value_ref.refs_1_.refs_2_), custom_call_target="tpu_custom_call" | custom-call | flops 24000000000 | bytes 10000000 | tf_op jit(solution)/shard_map/cross_forward/pallas_call | solution.py:346
  142.6 46.8 %feed.1 = (bf16[1024,768]{1,0:T(8,128)(2,1)}, f32[1024,768]{1,0:T(8,128)}, bf16[1024,768]{1,0:T(8,128)(2,1)}, bf16[1024,768]{1,0:T(8,128)(2,1)}, f32[1,768]{1,0:...) custom-call(f32[1024,768]{1,0:T(8,128)} %copy-done.6, ...), custom_call_target="tpu_custom_call" | custom-call | flops 32000000000 | bytes 40000000 | tf_op jit(solution)/shard_map/feed/pallas_call | solution.py:568
  189.5 40.9 %cross_backward.1 = (bf16[1024,768]{1,0:T(8,128)(2,1)}, bf16[2048,768]{1,0:T(8,128)(2,1)}, bf16[2048,768]{1,0:T(8,128)(2,1)}, bf16[4,2,32,768]{3,2,1,0:T(8,128)(2,1)}) custom-call(bf16[1024,768]{1,0:T(8,128)(2,1)} %convolution_convert_fusion.2.query_ref.refs_0_, bf16[2048,1536]{1,0:T(8,128)(2,1)} %fusion.key_ref.value_ref.refs_1_.refs_2_, ...), custom_call_target="tpu_custom_call" | custom-call | flops 35999997952 | bytes 20000000 | tf_op jit(solution)/shard_map/cross_backward/pallas_call | solution.py:399
  230.3 13.5 %cross_close.1 = (f32[1024,768]{1,0:T(8,128)}, f32[1,768]{1,0:T(1,128)}, bf16[768,768]{1,0:T(8,128)(2,1)}, bf16[768,768]{1,0:T(8,128)(2,1)}, bf16[1024,768]{1,0:T(8,128)(2,1)}, /*index=5*/bf16[1024,768]{1,0:T(8,128)(2,1)}) custom-call(f32[1024,768]{1,0:T(8,128)} %copy-done.6, f32[1024,768]{1,0:T(8,128)} %get-tuple-element.76.refs_1_, ...), custom_call_target="tpu_custom_call" | custom-call | flops 8000000000 | bytes 25000000 | tf_op jit(solution)/shard_map/cross_close/pallas_call | solution.py:682
  243.9 16.7 %memory_close.1 = (f32[2048,768]{1,0:T(8,128)}, bf16[768,768]{1,0:T(8,128)(2,1)}, bf16[768,768]{1,0:T(8,128)(2,1)}) custom-call(bf16[2048,768]{1,0:T(8,128)(2,1)} %bitcast.76, bf16[2048,768]{1,0:T(8,128)(2,1)} %get-tuple-element.88.key_grad_ref, bf16[2048,768]{1,0:T(8,128)(2,1)} %get-tuple-element.89.value_grad_ref, ...), custom_call_target="tpu_custom_call" | custom-call | flops 10000000000 | bytes 18000000 | tf_op jit(solution)/shard_map/memory_close/pallas_call | solution.py:734
  260.6 31.9 %self_backward.1 = (bf16[1024,768]{1,0:T(8,128)(2,1)}, bf16[1024,768]{1,0:T(8,128)(2,1)}, bf16[1024,768]{1,0:T(8,128)(2,1)}, f32[6,2,1024]{2,1,0:T(2,128)}, bf16[4,2,48,768]{3,2,1,0:T(8,128)(2,1)}) custom-call(s32[2]{0:T(128)} %refs_0_.3, bf16[1024,2304]{1,0:T(8,128)(2,1)} %convolution_convert_fusion.1.query_ref.key_ref.value_ref.refs_1_.refs_2_.refs_3_, ...), custom_call_target="tpu_custom_call" | custom-call | flops 24000000000 | bytes 20000000 | tf_op jit(solution)/shard_map/self_backward/pallas_call | solution.py:433
  292.5 0.8 reshape.121
  293.4 0.6 fusion.12
  294.2 2.1 copy.59
  296.3 18.9 %self_close.1 = (f32[1024,768]{1,0:T(8,128)}, f32[1,768]{1,0:T(1,128)}, bf16[768,768]{1,0:T(8,128)(2,1)}, bf16[768,768]{1,0:T(8,128)(2,1)}, bf16[768,768]{1,0:T(8,128)(2,1)}, /*index=5*/bf16[768,768]{1,0:T(8,128)(2,1)}) custom-call(bf16[1024,768]{1,0:T(8,128)(2,1)} %bitcast.60, f32[1024,768]{1,0:T(8,128)} %get-tuple-element.82.refs_1_, ...), custom_call_target="tpu_custom_call" | custom-call | flops 8000000000 | bytes 25000000 | tf_op jit(solution)/shard_map/self_close/pallas_call | solution.py:682
  315.2 1.3 select_maximum_fusion.refs_6_
  316.5 58.3 %fast_reduce.1 = (f32[4,96,192]{2,1,0:T(8,128)}, f32[4,64,192]{2,1,0:T(8,128)}, f32[4,96,192]{2,1,0:T(8,128)}, f32[8,768]{1,0:T(8,128)}) custom-call(bf16[4,2,48,768]{3,2,1,0:T(8,128)(2,1)} %get-tuple-element.99.refs_0_, bf16[4,2,32,768]{3,2,1,0:T(8,128)(2,1)} %get-tuple-element.100.refs_1_, bf16[768,768]{1,0:T(8,128)(2,1)} %get-tuple-element.101.refs_2_, ...), custom_call_target="tpu_custom_call" | custom-call | tf_op jit(solution)/shard_map/fast_reduce/pallas_call | solution.py:1446
  374.8 1.7 copy.51
  376.6 0.8 constant_dynamic-slice_fusion
  378.4 2.1 slice_bitcast_fusion
  380.4 1.3 reshape.124
  381.8 1.2 slice_reduce_fusion
  383.0 0.7 copy.56
  383.7 0.7 copy.57
  (41 shorter events, 3.7 us)
Async XLA Ops:
  7.2 61.5 %copy-start = (bf16[2,512,768]{2,1,0:T(8,128)(2,1)S(1)}, bf16[2,512,768]{2,1,0:T(8,128)(2,1)}, u32[]{:S(2)}) copy-start(bf16[2,512,768]{2,1,0:T(8,128)(2,1)} %param.20) | copy-start | bytes 4718596
  7.2 63.8 %copy-start.2 = (s32[1023]{0:T(1024)S(1)}, s32[1023]{0:T(1024)}, u32[]{:S(2)}) copy-start(s32[1023]{0:T(1024)} %param.23) | copy-start | bytes 12280
  7.2 135.4 %all-gather.2.cloned.1.call-start = ((), (), s32[]{:S(2)}) async-start(), calls=%async_computation.2 | async-start | bytes 7077888 | tf_op jit(solution)/shard_map/all_gather | solution.py:1472
  68.4 225.7 %reduce-scatter.5.cloned.1.call-start = ((), (), s32[]{:S(2)}) async-start(), calls=%async_computation.3 | async-start | bytes 7077888 | tf_op jit(solution)/shard_map/reduce_scatter | solution.py:1482
  108.6 5.0 %copy-start.6 = (f32[1024,768]{1,0:T(8,128)}, f32[1024,768]{1,0:T(8,128)S(1)}, u32[]{:S(2)}) copy-start(f32[1024,768]{1,0:T(8,128)S(1)} %get-tuple-element.169.middle_ref.refs_0_) | copy-start | bytes 9437188
  108.6 5.0 %copy-start.5 = (bf16[2,1024,768]{2,1,0:T(8,128)(2,1)S(1)}, bf16[2,1024,768]{2,1,0:T(8,128)(2,1)}, u32[]{:S(2)}) copy-start(bf16[2,1024,768]{2,1,0:T(8,128)(2,1)} %param.21) | copy-start | bytes 9437188
  189.4 191.1 %reduce-scatter.7.cloned.1.call-start = ((), (), s32[]{:S(2)}) async-start(), calls=%async_computation.4 | async-start | bytes 983040
  260.6 32.8 %copy-start.1 = (s32[1024]{0:T(1024)S(1)}, s32[1024]{0:T(1024)}, u32[]{:S(2)}) copy-start(s32[1024]{0:T(1024)} %pad.27) | copy-start | bytes 12292
  296.3 18.9 %copy-start.3 = (f32[1,768]{1,0:T(1,128)S(1)}, f32[1,768]{1,0:T(1,128)}, u32[]{:S(2)}) copy-start(f32[1,768]{1,0:T(1,128)} %get-tuple-element.107) | copy-start | bytes 9220
  296.3 18.9 %copy-start.4 = (f32[1,768]{1,0:T(1,128)S(1)}, f32[1,768]{1,0:T(1,128)}, u32[]{:S(2)}) copy-start(f32[1,768]{1,0:T(1,128)} %get-tuple-element.106) | copy-start | bytes 9220
Sparse Core Ops, SparseCore 0:
  68.6 63.9 all-gather.1
  189.5 69.2 reduce-scatter.4
  296.4 25.5 reduce-scatter.6

commit v3 on v2

--- a/solution.py
+++ b/solution.py
@@ -465,7 +465,7 @@
     )(prefix, qkv, qkv, qkv, upstream, context, lse, bias, *group)
 
 
-FEED_BLOCK = 256
+FEED_BLOCK = 512
 
 
 def feed_kernel(
@@ -665,7 +665,7 @@
 def run_close(values, carry, gain, left, right, grads, weights, project, name):
     rows, width = values.shape
     count = len(grads)
-    block = 512
+    block = 256
     wide = spec((block, width), lambda i: (i, 0))
 
     def columns(index):
@@ -724,7 +724,7 @@
 
 def run_memory(memory, key_grad, value_grad, weights, key_block, value_block):
     rows, width = memory.shape
-    block = 1024
+    block = 512
     wide = spec((block, width), lambda i: (i, 0))
     square = spec((width, width), lambda i: (0, 0))
 
@@ -1265,9 +1265,19 @@
                 copy.start()
             gathered[place.rep] = parts[place.rep]
 
-    def send(z):
-        line_send(z, 0)
-        line_send(z, 1)
+    def head(z):
+        if z > 0:
+            pl.when(place.z == 0)(functools.partial(line_send, z, 0))
+        if z < line - 1:
+            pl.when(place.z == line - 1)(functools.partial(line_send, z, 1))
+
+    def relay(hop, far):
+        up = [line - 1] if far else range(line - 2, hop, -1)
+        down = [0] if far else range(1, line - 1 - hop)
+        for z in up:
+            pl.when(place.z == hop)(functools.partial(line_send, z, 0))
+        for z in down:
+            pl.when(place.z == line - 1 - hop)(functools.partial(line_send, z, 1))
 
     def close():
         for z in range(line):
@@ -1284,7 +1294,7 @@
                 ahead = place.z < z if side == 0 else place.z > z
                 pl.when(ahead)(lambda: along(z, side).wait_send())
 
-    return load, send, close, drain
+    return load, head, relay, close, drain
 
 
 class VectorSum:
@@ -1393,36 +1403,50 @@
     start, pair_add, first_add, second_add, drain = plane_steps(
         place, shape, sources, line_scratch[0], plane_scratch
     )
-    _, send, close, line_drain = line_steps(place, shape, None, out, line_scratch)
+    _, head, relay, close, line_drain = line_steps(place, shape, None, out, line_scratch)
     vector = VectorSum(place, vector_ref, vector_out, scratch)
     for z in order:
         start(z)
     for load, *_ in plans:
         load().start()
     vector.round(0)
-    for index, z in enumerate(order):
-        pair_add(z)
+    pair_add(order[0])
     for load, *_ in plans:
         load().wait()
+    for z in order:
+        for _, ready_head, *_ in plans:
+            ready_head(z)
+    for z in order[1:]:
+        pair_add(z)
     vector.round(1)
-    for index, z in enumerate(order):
-        for _, ready_send, _, _ in plans:
-            ready_send(z)
+    for z in order[:2]:
         first_add(z)
-        if index == 1:
-            vector.round(2)
-    for _, _, ready_close, _ in plans:
+    for _, _, ready_relay, *_ in plans:
+        ready_relay(1, True)
+    vector.round(2)
+    for z in order[2:]:
+        first_add(z)
+    for hop in range(2, line - 1):
+        for _, _, ready_relay, *_ in plans:
+            ready_relay(hop, True)
+    for hop in range(1, line - 1):
+        for _, _, ready_relay, *_ in plans:
+            ready_relay(hop, False)
+    vector.round(3)
+    for z in order:
+        second_add(z)
+        head(z)
+    relay(1, True)
+    for _, _, _, ready_close, _ in plans:
         ready_close()
-    vector.round(3)
-    for index, z in enumerate(order):
-        second_add(z)
-        if index > 0:
-            send(order[index - 1])
-    send(order[-1])
+    for hop in range(2, line - 1):
+        relay(hop, True)
+    for hop in range(1, line - 1):
+        relay(hop, False)
     vector.round(4)
     close()
     vector.round(5)
-    for _, _, _, ready_drain in plans:
+    for *_, ready_drain in plans:
         ready_drain()
     line_drain()
     for z in order:

time: 395 us -> 377 us (0.954)
  Pallas kernels: 330 us -> 314 us
    pallas_call x1, Pallas kernels: 58.3 us -> 46.7 us  [fast_reduce(): pl.pallas_call(functools.partial(reduce_kernel, ready_shapes, shape, line...]
  transfers between devices with their start and end apart: 3 -> 3, of which waited for: 0 -> 0; matrix products, arithmetic and copies ran while one was open for 9% -> 10% of each run, Pallas kernels for 58% -> 57%
where the time goes in v3:
time: 377 us; the launch traced here: 373 us
  Pallas kernels  314 us (83%)
  matrix products  26.1 us (7%)
  local copies, waits for them, and re-layouts  14.8 us (4%)
  between operations  14.1 us (4%)
  other arithmetic  4.46 us (1%)
    pallas_call x1, Pallas kernels, fast_gather(): pl.pallas_call(functools.partial(gather_kernel, shapes, line), in_specs=[...  56.9 us
    pallas_call x1, Pallas kernels, fast_reduce(): pl.pallas_call(functools.partial(reduce_kernel, ready_shapes, shape, line...  46.7 us
    pallas_call x1, Pallas kernels, run_feed(): pl.pallas_call(feed_kernel, grid=(blocks,), in_specs=[whole(rows, **once)...  44.4 us
    pallas_call x1, Pallas kernels, run_cross_backward(): pl.pallas_call(kernel, grid=(nseq, PAIRS), in_specs=[rows, wide, spec((co...  40.9 us
    pallas_call x1, Pallas kernels, run_self_backward(): pl.pallas_call(kernel, grid_spec=pltpu.PrefetchScalarGridSpec(num_scalar_...  31.7 us
    pallas_call x2, Pallas kernels, run_close(): pl.pallas_call(functools.partial(close_kernel, count, project is not None...  31.3 us
    dot_general x4, matrix products, matmul(): return jnp.dot(left_side, right_side, preferred_element_type=F32)  24.4 us
    pallas_call x1, Pallas kernels, run_cross_forward(): pl.pallas_call(cross_forward, grid=(nseq, PAIRS), in_specs=[spec((length,...  20.4 us
  transfers between devices with their start and end apart: 3, of which 0 were waited for; matrix products, arithmetic and copies ran while one was open for 10% of the time, Pallas kernels for 57%

profile of v3, /device:TPU:0, one launch (start us, length us, event | category | flops | bytes accessed | tf_op | source)
XLA Modules:
  0.0 373.4 jit_solution(13664486441067985332)
XLA Ops:
  7.3 0.8 pad_bitcast_fusion
  8.0 0.7 pad_maximum_fusion.1
  8.8 0.6 pad.25.refs_3_.refs_9_
  9.5 2.0 pad_maximum_fusion
  11.5 56.9 %fast_gather.1 = (bf16[768,2560]{1,0:T(8,128)(2,1)}, bf16[768,4096]{1,0:T(8,128)(2,1)}, bf16[2048,768]{1,0:T(8,128)(2,1)}) custom-call(bf16[96,768]{1,0:T(8,128)(2,1)} %refs_0_.2, bf16[96,768]{1,0:T(8,128)(2,1)} %refs_1_.1, bf16[96,768]{1,0:T(8,128)(2,1)} %refs_2_.1, bf16[96,256]{1,0:T(8,128)(2,1)} %pad.25.refs_3_.refs_9_, bf16[96,768]{1,0:T(8,128)(2,1)} %refs_4_.1, ...), custom_call_target="tpu_custom_call" | custom-call | tf_op jit(solution)/shard_map/fast_gather/pallas_call | solution.py:1016
  69.1 1.1 fusion.17
  70.4 0.6 pad.26.table_ref
  71.2 0.6 pad.27
  71.8 5.1 %skewed_bias.1.bias_ref.refs_7_ = f32[12,128,896]{2,1,0:T(8,128)} custom-call(bf16[16,32]{1,0:T(8,128)(2,1)} %pad.26.table_ref, s32[1,1024]{1,0:T(1,128)} %bitcast.65), custom_call_target="tpu_custom_call" | custom-call | tf_op jit(solution)/shard_map/skewed_bias/pallas_call | solution.py:94
  76.9 0.6 slice_reduce_fusion
  77.4 7.6 %convolution_convert_fusion.1.query_ref.key_ref.value_ref.refs_1_.refs_2_.refs_3_ = bf16[1024,2304]{1,0:T(8,128)(2,1)} fusion(bf16[768,2560]{1,0:T(8,128)(2,1)} %get-tuple-element.69.refs_8_.refs_9_.refs_10_, bf16[1024,768]{1,0:T(8,128)(2,1)S(1)} %bitcast.61, f32[768]{0:T(1024)S(1)} %get-tuple-element.169, f32[1024]{0:T(1024)S(1)} %bitcast.68), kind=kOutput, calls=%fused_computation.2 | convolution fusion | flops 3629383680 | bytes 9837568 | tf_op jit(solution)/shard_map/dot_general | solution.py:28
  85.1 20.2 %self_forward.1 = (bf16[1024,768]{1,0:T(8,128)(2,1)}, f32[2,6,2,512]{3,2,1,0:T(2,128)}) custom-call(s32[2]{0:T(128)} %refs_0_.3, bf16[1024,2304]{1,0:T(8,128)(2,1)} %convolution_convert_fusion.1.query_ref.key_ref.value_ref.refs_1_.refs_2_.refs_3_, bf16[1024,2304]{1,0:T(8,128)(2,1)} %convolution_convert_fusion.1.query_ref.key_ref.value_ref.refs_1_.refs_2_.refs_3_, ...), custom_call_target="tpu_custom_call" | custom-call | flops 20000000000 | bytes 12000000 | tf_op jit(solution)/shard_map/self_forward/pallas_call | solution.py:316
  105.3 3.3 multiply_reduce_fusion
  108.6 5.0 %convolution_convert_fusion.2.query_ref.refs_0_ = bf16[1024,768]{1,0:T(8,128)(2,1)} fusion(f32[1024,768]{1,0:T(8,128)S(1)} %get-tuple-element.187.middle_ref.refs_0_, f32[768]{0:T(1024)S(1)} %get-tuple-element.168, f32[1024]{0:T(1024)S(1)} %add_rsqrt_fusion, bf16[768,4096]{1,0:T(8,128)(2,1)} %get-tuple-element.71.out_proj_ref.refs_6_.refs_7_.key_ref.value_ref), kind=kOutput, calls=%fused_computation.12 | convolution fusion | flops 1211105280 | bytes 5905408 | tf_op jit(solution)/shard_map/dot_general | solution.py:28
  113.6 8.5 %fusion.key_ref.value_ref.refs_1_.refs_2_ = bf16[2048,1536]{1,0:T(8,128)(2,1)} fusion(bf16[2048,768]{1,0:T(8,128)(2,1)S(1)} %bitcast.73, bf16[768,4096]{1,0:T(8,128)(2,1)} %get-tuple-element.71.out_proj_ref.refs_6_.refs_7_.key_ref.value_ref), kind=kOutput, calls=%fused_computation.1 | convolution fusion | flops 4834983936 | bytes 11796480 | tf_op jit(solution)/shard_map/dot_general | solution.py:28
  122.2 20.4 %cross_forward.1 = (bf16[1024,768]{1,0:T(8,128)(2,1)}, f32[2,6,2,512]{3,2,1,0:T(2,128)}) custom-call(bf16[1024,768]{1,0:T(8,128)(2,1)} %convolution_convert_fusion.2.query_ref.refs_0_, bf16[2048,1536]{1,0:T(8,128)(2,1)} %fusion.key_ref.value_ref.refs_1_.refs_2_, bf16[2048,1536]{1,0:T(8,128)(2,1)} %fusion.key_ref.value_ref.refs_1_.refs_2_), custom_call_target="tpu_custom_call" | custom-call | flops 24000000000 | bytes 10000000 | tf_op jit(solution)/shard_map/cross_forward/pallas_call | solution.py:346
  142.6 44.4 %feed.1 = (bf16[1024,768]{1,0:T(8,128)(2,1)}, f32[1024,768]{1,0:T(8,128)}, bf16[1024,768]{1,0:T(8,128)(2,1)}, bf16[1024,768]{1,0:T(8,128)(2,1)}, f32[1,768]{1,0:...) custom-call(f32[1024,768]{1,0:T(8,128)} %copy-done.6, ...), custom_call_target="tpu_custom_call" | custom-call | flops 32000000000 | bytes 40000000 | tf_op jit(solution)/shard_map/feed/pallas_call | solution.py:568
  187.1 40.9 %cross_backward.1 = (bf16[1024,768]{1,0:T(8,128)(2,1)}, bf16[2048,768]{1,0:T(8,128)(2,1)}, bf16[2048,768]{1,0:T(8,128)(2,1)}, bf16[4,2,32,768]{3,2,1,0:T(8,128)(2,1)}) custom-call(bf16[1024,768]{1,0:T(8,128)(2,1)} %convolution_convert_fusion.2.query_ref.refs_0_, bf16[2048,1536]{1,0:T(8,128)(2,1)} %fusion.key_ref.value_ref.refs_1_.refs_2_, ...), custom_call_target="tpu_custom_call" | custom-call | flops 35999997952 | bytes 20000000 | tf_op jit(solution)/shard_map/cross_backward/pallas_call | solution.py:399
  228.1 13.2 %cross_close.1 = (f32[1024,768]{1,0:T(8,128)}, f32[1,768]{1,0:T(1,128)}, bf16[768,768]{1,0:T(8,128)(2,1)}, bf16[768,768]{1,0:T(8,128)(2,1)}, bf16[1024,768]{1,0:T(8,128)(2,1)}, /*index=5*/bf16[1024,768]{1,0:T(8,128)(2,1)}) custom-call(f32[1024,768]{1,0:T(8,128)} %copy-done.6, f32[1024,768]{1,0:T(8,128)} %get-tuple-element.76.refs_1_, ...), custom_call_target="tpu_custom_call" | custom-call | flops 8000000000 | bytes 25000000 | tf_op jit(solution)/shard_map/cross_close/pallas_call | solution.py:682
  241.3 15.8 %memory_close.1 = (f32[2048,768]{1,0:T(8,128)}, bf16[768,768]{1,0:T(8,128)(2,1)}, bf16[768,768]{1,0:T(8,128)(2,1)}) custom-call(bf16[2048,768]{1,0:T(8,128)(2,1)} %bitcast.72, bf16[2048,768]{1,0:T(8,128)(2,1)} %get-tuple-element.88.key_grad_ref, bf16[2048,768]{1,0:T(8,128)(2,1)} %get-tuple-element.89.value_grad_ref, ...), custom_call_target="tpu_custom_call" | custom-call | flops 10000000000 | bytes 18000000 | tf_op jit(solution)/shard_map/memory_close/pallas_call | solution.py:734
  257.0 31.7 %self_backward.1 = (bf16[1024,768]{1,0:T(8,128)(2,1)}, bf16[1024,768]{1,0:T(8,128)(2,1)}, bf16[1024,768]{1,0:T(8,128)(2,1)}, f32[6,2,1024]{2,1,0:T(2,128)}, bf16[4,2,48,768]{3,2,1,0:T(8,128)(2,1)}) custom-call(s32[2]{0:T(128)} %refs_0_.3, bf16[1024,2304]{1,0:T(8,128)(2,1)} %convolution_convert_fusion.1.query_ref.key_ref.value_ref.refs_1_.refs_2_.refs_3_, ...), custom_call_target="tpu_custom_call" | custom-call | flops 24000000000 | bytes 20000000 | tf_op jit(solution)/shard_map/self_backward/pallas_call | solution.py:433
  288.7 0.8 reshape.130
  289.5 0.6 fusion.12
  290.3 2.1 copy.67
  292.5 18.1 %self_close.1 = (f32[1024,768]{1,0:T(8,128)}, f32[1,768]{1,0:T(1,128)}, bf16[768,768]{1,0:T(8,128)(2,1)}, bf16[768,768]{1,0:T(8,128)(2,1)}, bf16[768,768]{1,0:T(8,128)(2,1)}, /*index=5*/bf16[768,768]{1,0:T(8,128)(2,1)}) custom-call(bf16[1024,768]{1,0:T(8,128)(2,1)} %bitcast.60, f32[1024,768]{1,0:T(8,128)} %get-tuple-element.82.refs_1_, ...), custom_call_target="tpu_custom_call" | custom-call | flops 8000000000 | bytes 25000000 | tf_op jit(solution)/shard_map/self_close/pallas_call | solution.py:682
  310.6 1.3 select_maximum_fusion.refs_6_
  311.9 46.7 %fast_reduce.1 = (f32[4,96,192]{2,1,0:T(8,128)}, f32[4,64,192]{2,1,0:T(8,128)}, f32[4,96,192]{2,1,0:T(8,128)}, f32[8,768]{1,0:T(8,128)}) custom-call(bf16[4,2,48,768]{3,2,1,0:T(8,128)(2,1)} %get-tuple-element.99.refs_0_, bf16[4,2,32,768]{3,2,1,0:T(8,128)(2,1)} %get-tuple-element.100.refs_1_, bf16[768,768]{1,0:T(8,128)(2,1)} %get-tuple-element.101.refs_2_, ...), custom_call_target="tpu_custom_call" | custom-call | tf_op jit(solution)/shard_map/fast_reduce/pallas_call | solution.py:1470
  358.7 1.7 copy.57
  360.4 0.8 constant_dynamic-slice_fusion
  362.2 2.1 slice_bitcast_fusion
  364.3 1.3 reshape.133
  365.9 0.8 copy_bitcast_fusion
  (40 shorter events, 2.8 us)
Async XLA Ops:
  7.2 61.5 %copy-start = (bf16[2,512,768]{2,1,0:T(8,128)(2,1)S(1)}, bf16[2,512,768]{2,1,0:T(8,128)(2,1)}, u32[]{:S(2)}) copy-start(bf16[2,512,768]{2,1,0:T(8,128)(2,1)} %param.20) | copy-start | bytes 4718596
  7.2 63.8 %copy-start.2 = (s32[1023]{0:T(1024)S(1)}, s32[1023]{0:T(1024)}, u32[]{:S(2)}) copy-start(s32[1023]{0:T(1024)} %param.23) | copy-start | bytes 12280
  7.2 135.4 %all-gather.2.cloned.1.call-start = ((), (), s32[]{:S(2)}) async-start(), calls=%async_computation.2 | async-start | bytes 7077888 | tf_op jit(solution)/shard_map/all_gather | solution.py:1496
  68.4 221.9 %reduce-scatter.5.cloned.1.call-start = ((), (), s32[]{:S(2)}) async-start(), calls=%async_computation.3 | async-start | bytes 7077888 | tf_op jit(solution)/shard_map/reduce_scatter | solution.py:1506
  108.6 5.0 %copy-start.6 = (f32[1024,768]{1,0:T(8,128)}, f32[1024,768]{1,0:T(8,128)S(1)}, u32[]{:S(2)}) copy-start(f32[1024,768]{1,0:T(8,128)S(1)} %get-tuple-element.187.middle_ref.refs_0_) | copy-start | bytes 9437188
  108.6 5.0 %copy-start.5 = (bf16[2,1024,768]{2,1,0:T(8,128)(2,1)S(1)}, bf16[2,1024,768]{2,1,0:T(8,128)(2,1)}, u32[]{:S(2)}) copy-start(bf16[2,1024,768]{2,1,0:T(8,128)(2,1)} %param.21) | copy-start | bytes 9437188
  187.1 177.2 %reduce-scatter.7.cloned.1.call-start = ((), (), s32[]{:S(2)}) async-start(), calls=%async_computation.4 | async-start | bytes 983040
  257.0 32.5 %copy-start.1 = (s32[1024]{0:T(1024)S(1)}, s32[1024]{0:T(1024)}, u32[]{:S(2)}) copy-start(s32[1024]{0:T(1024)} %pad.27) | copy-start | bytes 12292
  292.4 18.2 %copy-start.3 = (f32[1,768]{1,0:T(1,128)S(1)}, f32[1,768]{1,0:T(1,128)}, u32[]{:S(2)}) copy-start(f32[1,768]{1,0:T(1,128)} %get-tuple-element.107) | copy-start | bytes 9220
  292.4 18.2 %copy-start.4 = (f32[1,768]{1,0:T(1,128)S(1)}, f32[1,768]{1,0:T(1,128)}, u32[]{:S(2)}) copy-start(f32[1,768]{1,0:T(1,128)} %get-tuple-element.106) | copy-start | bytes 9220
Sparse Core Ops, SparseCore 0:
  68.6 63.8 all-gather.1
  187.2 69.2 reduce-scatter.4
  292.6 25.5 reduce-scatter.6

commit v4 on v3

--- a/solution.py
+++ b/solution.py
@@ -1080,8 +1080,8 @@
         return [
             pltpu.VMEM(self.total_shape(line), BF16),
             pltpu.VMEM((2,) + self.total_shape(line), BF16),
-            pltpu.VMEM((4, self.part_rows, self.part_columns), F32),
-            pltpu.VMEM((4, self.part_rows, self.part_columns), F32),
+            pltpu.VMEM((4, self.part_rows, self.part_columns), BF16),
+            pltpu.VMEM((4, self.part_rows, self.part_columns), BF16),
             dma((1,)),
             dma((2, 2, line)),
             dma((2, 3)),
@@ -1257,7 +1257,8 @@
             if shape.exchange:
                 width = shape.part_columns
                 for index in range(4):
-                    parts[index, at, :] = result[:, index * width : (index + 1) * width]
+                    part = result[:, index * width : (index + 1) * width]
+                    parts[index, at, :] = part.astype(BF16)
             else:
                 out[at, :] = result
         if shape.exchange:
@@ -1288,7 +1289,7 @@
         if shape.exchange:
             for copy in swaps():
                 copy.wait()
-            out[...] = gathered[...]
+            out[...] = gathered[...].astype(F32)
         for z in range(line):
             for side in range(2):
                 ahead = place.z < z if side == 0 else place.z > z
@@ -1444,10 +1445,10 @@
     for hop in range(1, line - 1):
         relay(hop, False)
     vector.round(4)
+    for *_, ready_drain in plans:
+        ready_drain()
     close()
     vector.round(5)
-    for *_, ready_drain in plans:
-        ready_drain()
     line_drain()
     for z in order:
         drain(z)
@@ -1700,9 +1701,12 @@
         ((0, 4), (0, 0)),
     )
     pair_grad = lax.psum_scatter(pair_split, "rep").astype(F32)
-    pair_grad = pair_grad.reshape(shard, -1, 2, FEED_BLOCK)
-    gate_weight_grad = pair_grad[:, :, 0].reshape(shard, -1)
-    up_weight_grad = pair_grad[:, :, 1].reshape(shard, -1)
+    pieces = [
+        pair_grad[:, start : start + FEED_BLOCK]
+        for start in range(0, pair_grad.shape[1], FEED_BLOCK)
+    ]
+    gate_weight_grad = jnp.concatenate(pieces[0::2], axis=1)
+    up_weight_grad = jnp.concatenate(pieces[1::2], axis=1)
     down_weight_grad, (cross_out_grads, self_out_grads), totals = scatter_last(
         (down_term, down_sums), (cross_terms, cross_sums), self_terms, vector_block, 3
     )

time: 377 us -> 375 us (level)
  no operation moved by 1% of the time
where the time goes in v4:
time: 375 us; the launch traced here: 372 us
  Pallas kernels  312 us (83%)
  matrix products  26.1 us (7%)
  between operations  14.1 us (4%)
  local copies, waits for them, and re-layouts  13.2 us (4%)
  other arithmetic  5.41 us (1%)
    pallas_call x1, Pallas kernels, fast_gather(): pl.pallas_call(functools.partial(gather_kernel, shapes, line), in_specs=[...  56.9 us
    pallas_call x1, Pallas kernels, fast_reduce(): pl.pallas_call(functools.partial(reduce_kernel, ready_shapes, shape, line...  45.7 us
    pallas_call x1, Pallas kernels, run_feed(): pl.pallas_call(feed_kernel, grid=(blocks,), in_specs=[whole(rows, **once)...  44.4 us
    pallas_call x1, Pallas kernels, run_cross_backward(): pl.pallas_call(kernel, grid=(nseq, PAIRS), in_specs=[rows, wide, spec((co...  40.9 us
    pallas_call x1, Pallas kernels, run_self_backward(): pl.pallas_call(kernel, grid_spec=pltpu.PrefetchScalarGridSpec(num_scalar_...  31.7 us
    pallas_call x2, Pallas kernels, run_close(): pl.pallas_call(functools.partial(close_kernel, count, project is not None...  31.4 us
    dot_general x4, matrix products, matmul(): return jnp.dot(left_side, right_side, preferred_element_type=F32)  24.4 us
    pallas_call x1, Pallas kernels, run_cross_forward(): pl.pallas_call(cross_forward, grid=(nseq, PAIRS), in_specs=[spec((length,...  20.4 us
  transfers between devices with their start and end apart: 3, of which 0 were waited for; matrix products, arithmetic and copies ran while one was open for 10% of the time, Pallas kernels for 57%

profile of v4, /device:TPU:0, one launch (start us, length us, event | category | flops | bytes accessed | tf_op | source)
XLA Modules:
  0.0 371.7 jit_solution(2504423865616088938)
XLA Ops:
  7.3 0.8 pad_bitcast_fusion
  8.0 0.7 pad_maximum_fusion.1
  8.8 0.6 pad.25.refs_3_.refs_9_
  9.5 2.0 pad_maximum_fusion
  11.5 56.9 %fast_gather.1 = (bf16[768,2560]{1,0:T(8,128)(2,1)}, bf16[768,4096]{1,0:T(8,128)(2,1)}, bf16[2048,768]{1,0:T(8,128)(2,1)}) custom-call(bf16[96,768]{1,0:T(8,128)(2,1)} %refs_0_.2, bf16[96,768]{1,0:T(8,128)(2,1)} %refs_1_.1, bf16[96,768]{1,0:T(8,128)(2,1)} %refs_2_.1, bf16[96,256]{1,0:T(8,128)(2,1)} %pad.25.refs_3_.refs_9_, bf16[96,768]{1,0:T(8,128)(2,1)} %refs_4_.1, ...), custom_call_target="tpu_custom_call" | custom-call | tf_op jit(solution)/shard_map/fast_gather/pallas_call | solution.py:1016
  69.1 1.1 fusion.17
  70.4 0.6 pad.26.table_ref
  71.2 0.6 pad.27
  71.8 5.1 %skewed_bias.1.bias_ref.refs_7_ = f32[12,128,896]{2,1,0:T(8,128)} custom-call(bf16[16,32]{1,0:T(8,128)(2,1)} %pad.26.table_ref, s32[1,1024]{1,0:T(1,128)} %bitcast.64), custom_call_target="tpu_custom_call" | custom-call | tf_op jit(solution)/shard_map/skewed_bias/pallas_call | solution.py:94
  76.9 0.6 slice_reduce_fusion
  77.4 7.6 %convolution_convert_fusion.1.query_ref.key_ref.value_ref.refs_1_.refs_2_.refs_3_ = bf16[1024,2304]{1,0:T(8,128)(2,1)} fusion(bf16[768,2560]{1,0:T(8,128)(2,1)} %get-tuple-element.69.refs_8_.refs_9_.refs_10_, bf16[1024,768]{1,0:T(8,128)(2,1)S(1)} %bitcast.60, f32[768]{0:T(1024)S(1)} %get-tuple-element.151, f32[1024]{0:T(1024)S(1)} %bitcast.67), kind=kOutput, calls=%fused_computation.2 | convolution fusion | flops 3629383680 | bytes 9837568 | tf_op jit(solution)/shard_map/dot_general | solution.py:28
  85.1 20.2 %self_forward.1 = (bf16[1024,768]{1,0:T(8,128)(2,1)}, f32[2,6,2,512]{3,2,1,0:T(2,128)}) custom-call(s32[2]{0:T(128)} %refs_0_.3, bf16[1024,2304]{1,0:T(8,128)(2,1)} %convolution_convert_fusion.1.query_ref.key_ref.value_ref.refs_1_.refs_2_.refs_3_, bf16[1024,2304]{1,0:T(8,128)(2,1)} %convolution_convert_fusion.1.query_ref.key_ref.value_ref.refs_1_.refs_2_.refs_3_, ...), custom_call_target="tpu_custom_call" | custom-call | flops 20000000000 | bytes 12000000 | tf_op jit(solution)/shard_map/self_forward/pallas_call | solution.py:316
  105.3 3.3 multiply_reduce_fusion
  108.6 5.0 %convolution_convert_fusion.2.query_ref.refs_0_ = bf16[1024,768]{1,0:T(8,128)(2,1)} fusion(f32[1024,768]{1,0:T(8,128)S(1)} %get-tuple-element.169.middle_ref.refs_0_, f32[768]{0:T(1024)S(1)} %get-tuple-element.150, f32[1024]{0:T(1024)S(1)} %add_rsqrt_fusion, bf16[768,4096]{1,0:T(8,128)(2,1)} %get-tuple-element.71.out_proj_ref.refs_6_.refs_7_.key_ref.value_ref), kind=kOutput, calls=%fused_computation.12 | convolution fusion | flops 1211105280 | bytes 5905408 | tf_op jit(solution)/shard_map/dot_general | solution.py:28
  113.6 8.5 %fusion.key_ref.value_ref.refs_1_.refs_2_ = bf16[2048,1536]{1,0:T(8,128)(2,1)} fusion(bf16[2048,768]{1,0:T(8,128)(2,1)S(1)} %bitcast.72, bf16[768,4096]{1,0:T(8,128)(2,1)} %get-tuple-element.71.out_proj_ref.refs_6_.refs_7_.key_ref.value_ref), kind=kOutput, calls=%fused_computation.1 | convolution fusion | flops 4834983936 | bytes 11796480 | tf_op jit(solution)/shard_map/dot_general | solution.py:28
  122.1 20.4 %cross_forward.1 = (bf16[1024,768]{1,0:T(8,128)(2,1)}, f32[2,6,2,512]{3,2,1,0:T(2,128)}) custom-call(bf16[1024,768]{1,0:T(8,128)(2,1)} %convolution_convert_fusion.2.query_ref.refs_0_, bf16[2048,1536]{1,0:T(8,128)(2,1)} %fusion.key_ref.value_ref.refs_1_.refs_2_, bf16[2048,1536]{1,0:T(8,128)(2,1)} %fusion.key_ref.value_ref.refs_1_.refs_2_), custom_call_target="tpu_custom_call" | custom-call | flops 24000000000 | bytes 10000000 | tf_op jit(solution)/shard_map/cross_forward/pallas_call | solution.py:346
  142.6 44.4 %feed.1 = (bf16[1024,768]{1,0:T(8,128)(2,1)}, f32[1024,768]{1,0:T(8,128)}, bf16[1024,768]{1,0:T(8,128)(2,1)}, bf16[1024,768]{1,0:T(8,128)(2,1)}, f32[1,768]{1,0:...) custom-call(f32[1024,768]{1,0:T(8,128)} %copy-done.6, ...), custom_call_target="tpu_custom_call" | custom-call | flops 32000000000 | bytes 40000000 | tf_op jit(solution)/shard_map/feed/pallas_call | solution.py:568
  187.0 40.9 %cross_backward.1 = (bf16[1024,768]{1,0:T(8,128)(2,1)}, bf16[2048,768]{1,0:T(8,128)(2,1)}, bf16[2048,768]{1,0:T(8,128)(2,1)}, bf16[4,2,32,768]{3,2,1,0:T(8,128)(2,1)}) custom-call(bf16[1024,768]{1,0:T(8,128)(2,1)} %convolution_convert_fusion.2.query_ref.refs_0_, bf16[2048,1536]{1,0:T(8,128)(2,1)} %fusion.key_ref.value_ref.refs_1_.refs_2_, ...), custom_call_target="tpu_custom_call" | custom-call | flops 35999997952 | bytes 20000000 | tf_op jit(solution)/shard_map/cross_backward/pallas_call | solution.py:399
  228.0 13.2 %cross_close.1 = (f32[1024,768]{1,0:T(8,128)}, f32[1,768]{1,0:T(1,128)}, bf16[768,768]{1,0:T(8,128)(2,1)}, bf16[768,768]{1,0:T(8,128)(2,1)}, bf16[1024,768]{1,0:T(8,128)(2,1)}, /*index=5*/bf16[1024,768]{1,0:T(8,128)(2,1)}) custom-call(f32[1024,768]{1,0:T(8,128)} %copy-done.6, f32[1024,768]{1,0:T(8,128)} %get-tuple-element.76.refs_1_, ...), custom_call_target="tpu_custom_call" | custom-call | flops 8000000000 | bytes 25000000 | tf_op jit(solution)/shard_map/cross_close/pallas_call | solution.py:682
  241.2 15.8 %memory_close.1 = (f32[2048,768]{1,0:T(8,128)}, bf16[768,768]{1,0:T(8,128)(2,1)}, bf16[768,768]{1,0:T(8,128)(2,1)}) custom-call(bf16[2048,768]{1,0:T(8,128)(2,1)} %bitcast.71, bf16[2048,768]{1,0:T(8,128)(2,1)} %get-tuple-element.88.key_grad_ref, bf16[2048,768]{1,0:T(8,128)(2,1)} %get-tuple-element.89.value_grad_ref, ...), custom_call_target="tpu_custom_call" | custom-call | flops 10000000000 | bytes 18000000 | tf_op jit(solution)/shard_map/memory_close/pallas_call | solution.py:734
  257.0 31.7 %self_backward.1 = (bf16[1024,768]{1,0:T(8,128)(2,1)}, bf16[1024,768]{1,0:T(8,128)(2,1)}, bf16[1024,768]{1,0:T(8,128)(2,1)}, f32[6,2,1024]{2,1,0:T(2,128)}, bf16[4,2,48,768]{3,2,1,0:T(8,128)(2,1)}) custom-call(s32[2]{0:T(128)} %refs_0_.3, bf16[1024,2304]{1,0:T(8,128)(2,1)} %convolution_convert_fusion.1.query_ref.key_ref.value_ref.refs_1_.refs_2_.refs_3_, ...), custom_call_target="tpu_custom_call" | custom-call | flops 24000000000 | bytes 20000000 | tf_op jit(solution)/shard_map/self_backward/pallas_call | solution.py:433
  288.7 0.8 reshape.119
  289.5 0.6 fusion.12
  290.3 2.1 copy.56
  292.4 18.1 %self_close.1 = (f32[1024,768]{1,0:T(8,128)}, f32[1,768]{1,0:T(1,128)}, bf16[768,768]{1,0:T(8,128)(2,1)}, bf16[768,768]{1,0:T(8,128)(2,1)}, bf16[768,768]{1,0:T(8,128)(2,1)}, /*index=5*/bf16[768,768]{1,0:T(8,128)(2,1)}) custom-call(bf16[1024,768]{1,0:T(8,128)(2,1)} %bitcast.59, f32[1024,768]{1,0:T(8,128)} %get-tuple-element.82.refs_1_, ...), custom_call_target="tpu_custom_call" | custom-call | flops 8000000000 | bytes 25000000 | tf_op jit(solution)/shard_map/self_close/pallas_call | solution.py:682
  310.6 1.3 select_maximum_fusion.refs_6_
  311.9 45.7 %fast_reduce.1 = (f32[4,96,192]{2,1,0:T(8,128)}, f32[4,64,192]{2,1,0:T(8,128)}, f32[4,96,192]{2,1,0:T(8,128)}, f32[8,768]{1,0:T(8,128)}) custom-call(bf16[4,2,48,768]{3,2,1,0:T(8,128)(2,1)} %get-tuple-element.99.refs_0_, bf16[4,2,32,768]{3,2,1,0:T(8,128)(2,1)} %get-tuple-element.100.refs_1_, bf16[768,768]{1,0:T(8,128)(2,1)} %get-tuple-element.101.refs_2_, ...), custom_call_target="tpu_custom_call" | custom-call | tf_op jit(solution)/shard_map/fast_reduce/pallas_call | solution.py:1471
  357.6 1.7 copy.50
  359.4 0.8 constant_dynamic-slice_fusion
  361.2 2.1 slice_bitcast_fusion
  363.2 1.0 bitcast_convert_fusion
  364.2 0.8 fusion.22
  (39 shorter events, 2.5 us)
Async XLA Ops:
  7.2 61.5 %copy-start = (bf16[2,512,768]{2,1,0:T(8,128)(2,1)S(1)}, bf16[2,512,768]{2,1,0:T(8,128)(2,1)}, u32[]{:S(2)}) copy-start(bf16[2,512,768]{2,1,0:T(8,128)(2,1)} %param.20) | copy-start | bytes 4718596
  7.2 63.8 %copy-start.2 = (s32[1023]{0:T(1024)S(1)}, s32[1023]{0:T(1024)}, u32[]{:S(2)}) copy-start(s32[1023]{0:T(1024)} %param.23) | copy-start | bytes 12280
  7.2 135.3 %all-gather.2.cloned.1.call-start = ((), (), s32[]{:S(2)}) async-start(), calls=%async_computation.2 | async-start | bytes 7077888 | tf_op jit(solution)/shard_map/all_gather | solution.py:1497
  68.4 221.9 %reduce-scatter.5.cloned.1.call-start = ((), (), s32[]{:S(2)}) async-start(), calls=%async_computation.3 | async-start | bytes 7077888 | tf_op jit(solution)/shard_map/reduce_scatter | solution.py:1507
  108.6 5.0 %copy-start.6 = (f32[1024,768]{1,0:T(8,128)}, f32[1024,768]{1,0:T(8,128)S(1)}, u32[]{:S(2)}) copy-start(f32[1024,768]{1,0:T(8,128)S(1)} %get-tuple-element.169.middle_ref.refs_0_) | copy-start | bytes 9437188
  108.6 5.0 %copy-start.5 = (bf16[2,1024,768]{2,1,0:T(8,128)(2,1)S(1)}, bf16[2,1024,768]{2,1,0:T(8,128)(2,1)}, u32[]{:S(2)}) copy-start(bf16[2,1024,768]{2,1,0:T(8,128)(2,1)} %param.21) | copy-start | bytes 9437188
  187.0 176.3 %reduce-scatter.7.cloned.1.call-start = ((), (), s32[]{:S(2)}) async-start(), calls=%async_computation.4 | async-start | bytes 983040
  257.0 32.5 %copy-start.1 = (s32[1024]{0:T(1024)S(1)}, s32[1024]{0:T(1024)}, u32[]{:S(2)}) copy-start(s32[1024]{0:T(1024)} %pad.27) | copy-start | bytes 12292
  292.4 18.2 %copy-start.3 = (f32[1,768]{1,0:T(1,128)S(1)}, f32[1,768]{1,0:T(1,128)}, u32[]{:S(2)}) copy-start(f32[1,768]{1,0:T(1,128)} %get-tuple-element.107) | copy-start | bytes 9220
  292.4 18.2 %copy-start.4 = (f32[1,768]{1,0:T(1,128)S(1)}, f32[1,768]{1,0:T(1,128)}, u32[]{:S(2)}) copy-start(f32[1,768]{1,0:T(1,128)} %get-tuple-element.106) | copy-start | bytes 9220
Sparse Core Ops, SparseCore 0:
  68.6 63.9 all-gather.1
  187.1 69.2 reduce-scatter.4
  292.5 25.5 reduce-scatter.6
